TPU v7x, 512 devices: a whole 4x8x8 slice. The times are simulated.
512 devices in a mesh: src: 128 (over y, z, core), depth: 4 (over x).
Axes of the slice: x: 4, y: 8, z: 8, core: 2. Of those that a mesh axis runs over, the one named last changes fastest.
Arguments:
- incident: float32 [128, 4, 2, 4096], P('src'), may hold values from -6 to 6
- encode: int32 [128], P('src'), may hold values from 0 to 15
- freq_index: int32 [128], P('src'), may hold values from 0 to 7
- wavenum: float32 [8], replicated, may hold values from 1 to 2.8
- slowness: float32 [4, 4096], P('depth'), may hold values from -6 to 6
- probes: bfloat16 [64, 4, 4096], P(None, 'depth'), may hold values from -6 to 6
Outputs:
- sketch_basis: float32 [64, 4, 4096], P(None, 'depth', 'src')
- r_factor: float32 [64, 64], replicated
All inputs are finite; a program needn't handle non-finite values.
Results may differ from a plain program's by a relative error of at most 0.02.
Values may be sent and summed in bfloat16 or wider, within the bound.
A program may use at most 128 MiB of HBM per device.

v0:
```python
import math

import jax
import jax.numpy as jnp
from jax import lax
from jax.experimental import pallas as pl
from jax.experimental.pallas import tpu as pltpu
from jax.sharding import Mesh, PartitionSpec as P

SIDE = 64
CHIPS_Y = 8
CHIPS_Z = 8
CORES = 2
SRC_AXES = ("chip_y", "chip_z", "core")


DAMPING = 0.5
STEP_DEPTH = 1.0


def dft_tables(points, direction):
    counter = jnp.arange(points, dtype=jnp.int32)
    product = counter[:, None] * counter[None, :] % points
    angles = 2.0 * math.pi / points * product.astype(jnp.float32)
    cosine = jnp.cos(angles) / math.sqrt(points)
    sine_part = direction * jnp.sin(angles) / math.sqrt(points)
    matrix = jnp.stack(
        [jnp.stack([cosine, sine_part], axis=1), jnp.stack([-sine_part, cosine], axis=1)], axis=0
    )
    matrix = matrix.astype(jnp.bfloat16)
    total_points = points * points
    twist_index = counter[:, None] * counter[None, :] % total_points
    twist_angle = 2.0 * math.pi / total_points * twist_index.astype(jnp.float32)
    return (matrix, jnp.cos(twist_angle), direction * jnp.sin(twist_angle))


def transform(values, tables):
    matrix, twist_real, twist_imag = tables
    points = matrix.shape[1]
    leading = values.shape[:-3]
    grid_values = values.reshape((-1, 2, points, points))
    segmented = jnp.einsum(
        "nrab,rasc->nscb", grid_values, matrix, preferred_element_type=jnp.float32
    )
    real_part = segmented[:, 0]
    imag_part = segmented[:, 1]
    turned = jnp.stack(
        [
            real_part * twist_real - imag_part * twist_imag,
            real_part * twist_imag + imag_part * twist_real,
        ],
        axis=1,
    ).astype(jnp.bfloat16)
    result = jnp.einsum("nscb,sbtd->ntdc", turned, matrix, preferred_element_type=jnp.float32)
    return result.reshape(leading + (2, points, points))


def complex_times(first, second):
    real_part = first[..., 0, :, :] * second[..., 0, :, :] - first[..., 1, :, :] * second[..., 1, :, :]
    imag_part = first[..., 0, :, :] * second[..., 1, :, :] + first[..., 1, :, :] * second[..., 0, :, :]
    return jnp.stack([real_part, imag_part], axis=-3)


def conjugate(values):
    return jnp.stack([values[..., 0, :, :], -values[..., 1, :, :]], axis=-3)


def propagate(values, spectrum, forward, inverse):
    moved_on = transform(values.astype(jnp.bfloat16), forward)
    return transform(complex_times(moved_on, spectrum).astype(jnp.bfloat16), inverse)


def propagator(wave_nums, points_all):
    counter = jnp.arange(points_all, dtype=jnp.int32)
    folded = jnp.where(counter < points_all // 2, counter, counter - points_all).astype(jnp.float32)
    lateral = 2.0 * math.pi / points_all * folded
    excess = wave_nums[:, None] ** 2 - lateral[None, :] ** 2
    upward = jnp.sqrt(jnp.maximum(excess, 0.0)) * STEP_DEPTH
    damped = jnp.sqrt(jnp.maximum(-excess, 0.0)) * STEP_DEPTH
    real_part = jnp.where(excess > 0, jnp.cos(upward), jnp.exp(-damped))
    imag_part = jnp.where(excess > 0, jnp.sin(upward), jnp.zeros_like(upward))
    return jnp.stack([real_part, imag_part], axis=1)


def screens(wave_nums, slowness):
    phase = wave_nums[:, None, None] * STEP_DEPTH * slowness[None]
    return jnp.stack([jnp.cos(phase), jnp.sin(phase)], axis=2)


def encoded_sources(incident, encode, sources):
    shifts = jnp.arange(sources, dtype=jnp.int32)
    bit_set = encode[:, None] >> shifts[None, :] & 1
    signs_all = (1 - 2 * bit_set).astype(jnp.float32)
    return jnp.sum(signs_all[:, :, None, None] * incident, axis=1)


def lookup_waves(freq_index, wavenum, table_size):
    onehot_rows = (freq_index[:, None] == jnp.arange(table_size, dtype=jnp.int32)[None, :]).astype(
        jnp.float32
    )
    return jnp.sum(onehot_rows * wavenum[None, :], axis=1)


def gram_sum_kernel(stages, part_ref, out_ref, *scratch):
    count = len(stages)
    slots = scratch[:count]
    send_sems, recv_sems, carried = scratch[count], scratch[count + 1], scratch[count + 2]
    barrier = pltpu.get_barrier_semaphore()
    peers_total = 0
    for axis, size in stages:
        me = lax.axis_index(axis)
        for step in range(1, size):
            pl.semaphore_signal(barrier, inc=1, device_id={axis: lax.rem(me + step, size)},
                                device_id_type=pl.DeviceIdType.MESH)
            peers_total += 1
    pl.semaphore_wait(barrier, peers_total)
    carried[...] = part_ref[...]
    used = 0
    offset = 0
    for stage, (axis, size) in enumerate(stages):
        me = lax.axis_index(axis)
        slot = slots[stage]
        copies = []
        for step in range(1, size):
            copy = pltpu.make_async_remote_copy(
                src_ref=carried,
                dst_ref=slot.at[me],
                send_sem=send_sems.at[used + step - 1],
                recv_sem=recv_sems.at[offset + me],
                device_id={axis: lax.rem(me + step, size)},
                device_id_type=pl.DeviceIdType.MESH,
            )
            copy.start()
            copies.append(copy)
        slot[me] = carried[...]
        for copy in copies:
            copy.wait_send()
        for step in range(1, size):
            sender = lax.rem(me + size - step, size)
            incoming = pltpu.make_async_remote_copy(
                src_ref=carried,
                dst_ref=slot.at[sender],
                send_sem=send_sems.at[used + step - 1],
                recv_sem=recv_sems.at[offset + sender],
                device_id={axis: lax.rem(me + step, size)},
                device_id_type=pl.DeviceIdType.MESH,
            )
            incoming.wait_recv()
        used += size - 1
        offset += size
        total = slot[0]
        for member in range(1, size):
            total = total + slot[member]
        carried[...] = total
    out_ref[...] = carried[...]


def gram_sum(part, stages):
    stages = [(axis, size) for axis, size in stages if size > 1]
    sends = sum(size - 1 for _, size in stages)
    scratch = [pltpu.VMEM((size,) + part.shape, jnp.float32) for _, size in stages]
    scratch += [
        pltpu.SemaphoreType.DMA((max(sends, 1),)),
        pltpu.SemaphoreType.DMA((max(sum(size for _, size in stages), 1),)),
        pltpu.VMEM(part.shape, jnp.float32),
    ]
    return pl.pallas_call(
        lambda *refs: gram_sum_kernel(stages, *refs),
        out_shape=jax.ShapeDtypeStruct(part.shape, jnp.float32),
        in_specs=[pl.BlockSpec(memory_space=pltpu.VMEM)],
        out_specs=pl.BlockSpec(memory_space=pltpu.VMEM),
        scratch_shapes=scratch,
        compiler_params=pltpu.CompilerParams(collective_id=0, has_side_effects=True),
    )(part)


def exchange(axis, size, current, slot, send_sems, recv_sems, offset, whole=False):
    me = lax.axis_index(axis)
    copies = []
    for step in range(1, size):
        peer = lax.rem(me + step, size)
        copy = pltpu.make_async_remote_copy(
            src_ref=current if whole else current.at[peer],
            dst_ref=slot.at[me],
            send_sem=send_sems.at[offset + peer],
            recv_sem=recv_sems.at[offset + me],
            device_id={axis: peer},
            device_id_type=pl.DeviceIdType.MESH,
        )
        copy.start()
        copies.append(copy)
    for copy in copies:
        copy.wait_send()
    for step in range(1, size):
        sender = lax.rem(me + size - step, size)
        incoming = pltpu.make_async_remote_copy(
            src_ref=current if whole else current.at[sender],
            dst_ref=slot.at[sender],
            send_sem=send_sems.at[offset + sender],
            recv_sem=recv_sems.at[offset + sender],
            device_id={axis: sender},
            device_id_type=pl.DeviceIdType.MESH,
        )
        incoming.wait_recv()
    return me


def scatter_kernel(stages, part_ref, extra_ref, out_ref, *scratch):
    count = len(stages)
    slots = scratch[:count]
    sums = scratch[count : 2 * count - 1]
    mine, gathered, send_sems, recv_sems = scratch[2 * count - 1 :]
    barrier = pltpu.get_barrier_semaphore()
    peers_total = 0
    for axis, size in stages + [("depth", out_ref.shape[0])]:
        me = lax.axis_index(axis)
        for step in range(1, size):
            pl.semaphore_signal(barrier, inc=1, device_id={axis: lax.rem(me + step, size)},
                                device_id_type=pl.DeviceIdType.MESH)
            peers_total += 1
    pl.semaphore_wait(barrier, peers_total)
    current = part_ref
    offset = 0
    for stage, (axis, size) in enumerate(stages):
        me = exchange(axis, size, current, slots[stage], send_sems, recv_sems, offset)
        offset += size
        total = current[me]
        for step in range(1, size):
            total = total + slots[stage][lax.rem(me + size - step, size)]
        if stage + 1 < count:
            sums[stage][...] = total
            current = sums[stage]
        else:
            mine[0] = total
    mine[1] = extra_ref[...]
    depth_size = out_ref.shape[0]
    me = exchange("depth", depth_size, mine, gathered, send_sems, recv_sems, offset, whole=True)
    gathered[me] = mine[...]
    out_ref[...] = gathered[...]


def scatter_gather(part, extra, stages, depth_size):
    stages = [(axis, size) for axis, size in stages if size > 1]
    part = part.reshape(tuple(size for _, size in stages) + part.shape[-2:])
    scratch = [pltpu.VMEM(part.shape[stage:], jnp.float32) for stage in range(len(stages))]
    scratch += [pltpu.VMEM(part.shape[stage + 1 :], jnp.float32) for stage in range(len(stages) - 1)]
    block = (2,) + extra.shape
    scratch += [
        pltpu.VMEM(block, jnp.float32),
        pltpu.VMEM((depth_size,) + block, jnp.float32),
        pltpu.SemaphoreType.DMA((sum(size for _, size in stages) + depth_size,)),
        pltpu.SemaphoreType.DMA((sum(size for _, size in stages) + depth_size,)),
    ]
    return pl.pallas_call(
        lambda *refs: scatter_kernel(stages, *refs),
        out_shape=jax.ShapeDtypeStruct((depth_size,) + block, jnp.float32),
        in_specs=[pl.BlockSpec(memory_space=pltpu.VMEM)] * 2,
        out_specs=pl.BlockSpec(memory_space=pltpu.VMEM),
        scratch_shapes=scratch,
        compiler_params=pltpu.CompilerParams(collective_id=1, has_side_effects=True),
    )(part, extra)


def shards(incident, encode, freq_index, wavenum, slowness, probes):
    points_all = SIDE * SIDE
    forward = dft_tables(SIDE, -1.0)
    inverse = dft_tables(SIDE, 1.0)
    group_count = incident.shape[0]
    probe_count = probes.shape[0]
    src_count = lax.axis_size(SRC_AXES)
    depth_count = lax.axis_size("depth")
    spread = jnp.broadcast_to(slowness[None], (depth_count,) + slowness.shape)
    slowness_all = lax.all_to_all(spread, "depth", 0, 0, tiled=True).reshape(-1, slowness.shape[-1])
    plane_count = slowness_all.shape[0]
    probe_mine = lax.all_to_all(probes, "depth", 0, 1, tiled=True).astype(jnp.float32)
    probe_mine = probe_mine.reshape(probe_mine.shape[:2] + (SIDE, SIDE))
    sources = encoded_sources(incident, encode, incident.shape[1])
    sources = sources.reshape(sources.shape[:-1] + (SIDE, SIDE))
    wave_nums = lookup_waves(freq_index, wavenum, wavenum.shape[0])
    spectra = propagator(wave_nums, points_all)
    spectra = spectra.reshape(spectra.shape[:-1] + (SIDE, SIDE))
    spectra_back = conjugate(spectra)
    plane_screens = screens(wave_nums, slowness_all)
    plane_screens = plane_screens.reshape(plane_screens.shape[:-1] + (SIDE, SIDE))
    born_scale = wave_nums * STEP_DEPTH

    fields = []
    current = sources
    for plane in range(plane_count):
        current = complex_times(plane_screens[:, plane], propagate(current, spectra, forward, inverse))
        fields.append(current)

    def born(plane):
        scaled = born_scale[:, None, None, None] * probe_mine[None, :, plane]
        background = fields[plane]
        return jnp.stack([-scaled * background[:, None, 1], scaled * background[:, None, 0]], axis=2)

    tangent = born(0)
    for plane in range(1, plane_count):
        moved_on = complex_times(
            plane_screens[:, plane][:, None], propagate(tangent, spectra[:, None], forward, inverse)
        )
        tangent = moved_on + born(plane)

    adjoint = tangent
    pieces = [None] * plane_count
    for plane in reversed(range(plane_count)):
        background = fields[plane]
        product_terms = born_scale[:, None, None, None] * (
            background[:, None, 0] * adjoint[:, :, 1] - background[:, None, 1] * adjoint[:, :, 0]
        )
        pieces[plane] = jnp.sum(product_terms, axis=0)
        if plane > 0:
            turned_back = complex_times(conjugate(plane_screens[:, plane])[:, None], adjoint)
            adjoint = propagate(turned_back, spectra_back[:, None], forward, inverse)
    sketch_part = jnp.stack(pieces, axis=1)
    rows, planes = sketch_part.shape[0], sketch_part.shape[1]
    by_axes = sketch_part.reshape(rows, planes, CHIPS_Y, CHIPS_Z, CORES, -1)
    slab_width = by_axes.shape[-1]
    by_axes = jnp.transpose(by_axes, (4, 3, 2, 0, 1, 5)).reshape(
        CORES, CHIPS_Z, CHIPS_Y, rows, planes * slab_width
    )
    src_index = lax.axis_index(SRC_AXES)
    probe_slab = lax.dynamic_slice_in_dim(probes, src_index * slab_width, slab_width, 2)
    probe_slab = jnp.transpose(probe_slab.reshape(depth_count, rows, slab_width), (1, 0, 2))
    probe_slab = probe_slab.reshape(rows, depth_count * slab_width).astype(jnp.float32)
    stage_sizes = [("core", CORES), ("chip_z", CHIPS_Z), ("chip_y", CHIPS_Y)]
    both = scatter_gather(by_axes, probe_slab, stage_sizes, depth_count)
    summed = both[:, 0].reshape(probe_count, planes, slab_width)
    local_probes = jnp.transpose(
        both[:, 1].reshape(depth_count, rows, depth_count, slab_width), (2, 1, 0, 3)
    ).reshape(probe_count, planes, slab_width)
    sketch_all = summed / (group_count * src_count) + DAMPING * local_probes
    flattened_all = sketch_all.reshape(probe_count, -1)
    row_total = flattened_all.shape[1] * src_count
    gram_local = jnp.dot(flattened_all, flattened_all.T, precision=lax.Precision.HIGHEST) / row_total
    stage_sizes = [(axis, lax.axis_size(axis)) for axis in ("core", "chip_z", "chip_y")]
    gram_matrix = gram_sum(gram_local, stage_sizes)
    sketch = lax.dynamic_slice_in_dim(sketch_all, lax.axis_index("depth"), 1, 1)
    local_planes = 1
    flattened = sketch.reshape(probe_count, local_planes * slab_width)
    lower_factor = jnp.linalg.cholesky(gram_matrix)
    identity = jnp.eye(probe_count, dtype=jnp.float32)
    inverse_lower = lax.linalg.triangular_solve(lower_factor, identity, left_side=True, lower=True)
    sketch_basis = jnp.dot(inverse_lower, flattened, precision=lax.Precision.HIGHEST).reshape(
        probe_count, local_planes, slab_width
    )
    return (sketch_basis, lower_factor.T)


def solution(mesh):
    src_size, depth_size = mesh.devices.shape
    cut = mesh.devices.reshape(CHIPS_Y, CHIPS_Z, CORES, depth_size)
    fine = Mesh(cut, SRC_AXES + ("depth",))
    in_specs = (
        P(SRC_AXES, None, None, None),
        P(SRC_AXES),
        P(SRC_AXES),
        P(),
        P("depth", None),
        P(None, "depth", None),
    )
    out_specs = (P(None, "depth", SRC_AXES), P())
    return jax.shard_map(shards, mesh=fine, in_specs=in_specs, out_specs=out_specs, check_vma=False)
```

profile of v0, /device:TPU:1, one launch (start us, length us, event | category | flops | bytes accessed | tf_op | source)
XLA Modules:
  0.0 174.8 jit_solution(13881516947889377325)
XLA Ops:
  0.6 1.4 broadcast_in_dim.14
  2.0 4.8 %all-to-all-start = ((f32[4,1,4096]{2,1,0:T(1,128)}), f32[4,1,4096]{2,1,0:T(1,128)S(1)}, u32[]{:S(2)}, u32[]{:S(2)}) async-start(f32[4,1,4096]{2,1,0:T(1,128)} %broadcast_in_dim.14), calls=%async_computation | async-start | bytes 131072 | tf_op jit(solution)/shard_map/all_to_all | solution.py:273
  8.3 1.3 fusion.190
  11.8 1.0 multiply_reduce_fusion
  14.3 0.8 constant_dynamic-slice_fusion.1
  15.6 2.0 %reduce.13 = bf16[64,4096]{1,0:T(8,128)(2,1)S(1)} reduce(bf16[64,1,4096]{2,0,1:T(8,128)(2,1)} %param.11, bf16[]{:T(256)} %broadcast.1766), dimensions={1}, to_apply=%copy.267.reduce_sub_computation | reduce | bytes 1048578 | tf_op args[5]
  17.6 1.2 reshape.2018
  18.8 0.7 reshape.1918.refs_1_
  19.5 4.2 %all-to-all-start.1 = ((bf16[4,2,32768]{2,1,0:T(2,128)(2,1)}), bf16[4,2,32768]{2,1,0:T(2,128)(2,1)S(1)}, u32[]{:S(2)}, u32[]{:S(2)}) async-start(bf16[4,2,32768]{2,1,0:T(2,128)(2,1)} %reshape.2018), calls=%async_computation.1 | async-start | bytes 1048576 | tf_op jit(solution)/shard_map/all_to_all | solution.py:275
  23.7 2.8 %sine_reduce_fusion = (f32[4,4096]{1,0:T(4,128)S(1)}, f32[4,4096]{1,0:T(4,128)S(1)}) fusion(f32[4,1,4096]{2,1,0:T(1,128)S(1)} %all-to-all-done, f32[]{:T(128)} %fusion.190), kind=kLoop, calls=%fused_computation.240 | loop fusion | flops 16384 | bytes 196612 | tf_op jit(solution)/shard_map/sin | solution.py:87
  30.8 0.6 slice_bitcast_fusion.15
  32.9 0.6 copy.306
  33.6 0.6 copy.308
  37.9 0.6 slice_bitcast_fusion.17
  38.6 0.7 slice_bitcast_fusion.9
  39.3 0.7 reshape.2019
  40.0 0.7 copy.554
  40.8 1.0 reshape.1917
  41.8 1.9 %multiply_bitcast_fusion = (f32[1,16,1,64,64]{4,3,1,2,0:T(8,128)S(1)}, f32[16,1,64,64]{3,2,1,0:T(8,128)S(1)}, f32[16,1,64,64]{3,2,1,0:T(8,128)S(1)}, bf16[16,1,6...) fusion(f32[16,4,64,64]{3,2,1,0:T(8,128)S(1)} %reshape.1917, ...), kind=kLoop, calls=%fused_computation.165 | loop fusion | flops 1048576 | bytes 2736132 | tf_op jit(solution)/shard_map/stack | solution.py:296
  49.8 0.7 fusion.30
  51.3 1.2 fusion.69
  56.8 1.2 fusion.77
  60.8 1.6 squeeze.29
  62.4 1.6 squeeze.30
  64.1 2.7 %squeeze.31 = f32[16,1,8,8,2,32]{5,4,3,2,0,1:T(2,128)} reshape(f32[1,16,1,64,64]{4,3,1,2,0:T(8,128)} %get-tuple-element.84) | data formatting | bytes 524288 | tf_op jit(solution)/shard_map/squeeze | solution.py:59
  66.8 1.6 squeeze.32
  68.4 1.6 squeeze.33
  70.0 1.6 squeeze.34
  71.7 2.7 %squeeze.35 = f32[16,1,8,8,2,32]{5,4,3,2,0,1:T(2,128)} reshape(f32[1,16,1,64,64]{4,3,1,2,0:T(8,128)} %get-tuple-element.88) | data formatting | bytes 524288 | tf_op jit(solution)/shard_map/squeeze | solution.py:59
  74.4 2.3 %fusion.10 = f32[16,1,8,8,2,32]{5,3,4,2,1,0:T(8,128)S(1)} fusion(f32[16,1,8,8,2,32]{5,4,3,2,0,1:T(2,128)} %squeeze.29, f32[16,1,8,8,2,32]{5,4,3,2,0,1:T(2,128)S(1)} %squeeze.28, f32[8,8,2,32]{3,1,2,0:T(8,128)S(1)} %copy-done.13, f32[8,8,2,32]{3,1,2,0:T(8,128)S(1)} %copy-done.11, f32[]{:T(128)} %fusion.190), kind=kLoop, calls=%fused_computation.63 | loop fusion | flops 262144 | bytes 819204 | tf_op jit(solution)/shard_map/mul | solution.py:309
  76.8 2.0 %fusion.8 = f32[16,1,8,8,2,32]{5,3,4,2,1,0:T(8,128)S(1)} fusion(f32[16,1,8,8,2,32]{5,4,3,2,0,1:T(2,128)} %squeeze.31, f32[16,1,8,8,2,32]{5,4,3,2,0,1:T(2,128)S(1)} %squeeze.30, f32[8,8,2,32]{3,1,2,0:T(8,128)S(1)} %copy-done.15, f32[8,8,2,32]{3,1,2,0:T(8,128)S(1)} %copy-done.12, f32[]{:T(128)} %fusion.190), kind=kLoop, calls=%fused_computation.59 | loop fusion | flops 262144 | bytes 819204 | tf_op jit(solution)/shard_map/mul | solution.py:309
  78.8 1.6 fusion.6
  80.5 0.9 fusion.4
  81.9 4.7 %copy.320 = f32[2,8,8,16,4,32]{5,4,3,2,1,0:T(4,128)} copy(f32[2,8,8,16,4,32]{5,1,0,2,4,3:T(8,128)S(1)} %maximum_bitcast_fusion) | data formatting | bytes 2097152 | tf_op jit(solution)/shard_map/transpose | solution.py:320
  86.6 4.5 %reshape.1914.refs_0_ = f32[2,8,8,16,128]{4,3,2,1,0:T(8,128)} reshape(f32[2,8,8,16,4,32]{5,4,3,2,1,0:T(4,128)} %copy.320) | data formatting | bytes 2097152 | tf_op jit(solution)/shard_map/reshape | solution.py:320
  91.1 40.0 %shard_map.77 = f32[4,2,16,128]{3,2,1,0:T(8,128)} custom-call(f32[2,8,8,16,128]{4,3,2,1,0:T(8,128)} %reshape.1914.refs_0_, f32[16,128]{1,0:T(8,128)} %reshape.1918.refs_1_), custom_call_target="tpu_custom_call" | custom-call | tf_op jit(solution)/shard_map/pallas_call | solution.py:254
  131.1 0.8 slice_multiply_fusion.4
  132.2 0.8 slice_multiply_fusion.5
  133.2 0.9 fusion.refs_0_
  134.1 25.1 %shard_map.78 = f32[64,64]{1,0:T(8,128)} custom-call(f32[64,64]{1,0:T(8,128)} %fusion.refs_0_), custom_call_target="tpu_custom_call" | custom-call | tf_op jit(solution)/shard_map/pallas_call | solution.py:167
  159.3 0.8 copy.326
  160.1 0.8 fusion.147
  160.9 5.8 %cholesky.16 = f32[64,64]{1,0:T(8,128)S(1)} custom-call(f32[64,64]{1,0:T(8,128)S(1)} %fusion.147), custom_call_target="Cholesky" | custom-call | tf_op jit(solution)/shard_map/jit(cholesky)/cholesky | solution.py:342
  166.7 0.6 compare_reduce_fusion
  167.4 0.7 fusion.159
  168.0 4.9 %custom-call.6 = f32[1,64,64]{1,2,0:T(8,128)S(1)} custom-call(f32[1,64,64]{2,1,0:T(8,128)S(1)} %get-tuple-element.150), custom_call_target="InvertDiagBlocksLowerTriangular" | custom-call | tf_op jit(solution)/shard_map/triangular_solve | solution.py:344
  173.2 0.7 copy.328
  173.9 0.8 convolution_bitcast_fusion.41
  (191 shorter events, 27.1 us)
Async XLA Ops:
  2.0 17.5 %all-to-all-start = ((f32[4,1,4096]{2,1,0:T(1,128)}), f32[4,1,4096]{2,1,0:T(1,128)S(1)}, u32[]{:S(2)}, u32[]{:S(2)}) async-start(f32[4,1,4096]{2,1,0:T(1,128)} %broadcast_in_dim.14), calls=%async_computation | async-start | bytes 131072 | tf_op jit(solution)/shard_map/all_to_all | solution.py:273
  19.5 19.8 %all-to-all-start.1 = ((bf16[4,2,32768]{2,1,0:T(2,128)(2,1)}), bf16[4,2,32768]{2,1,0:T(2,128)(2,1)S(1)}, u32[]{:S(2)}, u32[]{:S(2)}) async-start(bf16[4,2,32768]{2,1,0:T(2,128)(2,1)} %reshape.2018), calls=%async_computation.1 | async-start | bytes 1048576 | tf_op jit(solution)/shard_map/all_to_all | solution.py:275
  26.9 12.3 %copy-start.3 = (f32[1,1,64,64]{3,2,1,0:T(8,128)}, f32[1,1,64,64]{3,2,1,0:T(8,128)S(1)}, u32[]{:S(2)}) copy-start(f32[1,1,64,64]{3,2,1,0:T(8,128)S(1)} %get-tuple-element.108) | copy-start | bytes 49156
  28.2 11.1 %copy-start.4 = (f32[1,1,64,64]{3,2,1,0:T(8,128)}, f32[1,1,64,64]{3,2,1,0:T(8,128)S(1)}, u32[]{:S(2)}) copy-start(f32[1,1,64,64]{3,2,1,0:T(8,128)S(1)} %get-tuple-element.19) | copy-start | bytes 49156
  28.2 11.1 %copy-start.5 = (f32[1,1,64,64]{3,2,1,0:T(8,128)}, f32[1,1,64,64]{3,2,1,0:T(8,128)S(1)}, u32[]{:S(2)}) copy-start(f32[1,1,64,64]{3,2,1,0:T(8,128)S(1)} %get-tuple-element.106) | copy-start | bytes 49156
  29.5 9.8 %copy-start.6 = (f32[1,1,64,64]{3,2,1,0:T(8,128)}, f32[1,1,64,64]{3,2,1,0:T(8,128)S(1)}, u32[]{:S(2)}) copy-start(f32[1,1,64,64]{3,2,1,0:T(8,128)S(1)} %get-tuple-element.17) | copy-start | bytes 49156
  29.5 9.8 %copy-start.7 = (f32[1,1,64,64]{3,2,1,0:T(8,128)}, f32[1,1,64,64]{3,2,1,0:T(8,128)S(1)}, u32[]{:S(2)}) copy-start(f32[1,1,64,64]{3,2,1,0:T(8,128)S(1)} %get-tuple-element.104) | copy-start | bytes 49156
  30.7 8.6 %copy-start.8 = (f32[1,1,64,64]{3,2,1,0:T(8,128)}, f32[1,1,64,64]{3,2,1,0:T(8,128)S(1)}, u32[]{:S(2)}) copy-start(f32[1,1,64,64]{3,2,1,0:T(8,128)S(1)} %get-tuple-element.96) | copy-start | bytes 49156
  30.7 8.6 %copy-start.9 = (f32[1,1,64,64]{3,2,1,0:T(8,128)}, f32[1,1,64,64]{3,2,1,0:T(8,128)S(1)}, u32[]{:S(2)}) copy-start(f32[1,1,64,64]{3,2,1,0:T(8,128)S(1)} %get-tuple-element.95) | copy-start | bytes 49156
  44.2 1.5 copy-start.22
  44.2 1.5 copy-start.23
  46.4 1.5 copy-start.20
  46.4 1.5 copy-start.21
  48.5 1.3 copy-start.10
  49.1 1.8 %copy-start.18 = (f32[64,64]{1,0:T(8,128)S(1)}, f32[64,64]{1,0:T(8,128)}, u32[]{:S(2)}) copy-start(f32[64,64]{1,0:T(8,128)} %get-tuple-element.100) | copy-start | bytes 49156
  49.1 1.8 %copy-start.19 = (f32[64,64]{1,0:T(8,128)S(1)}, f32[64,64]{1,0:T(8,128)}, u32[]{:S(2)}) copy-start(f32[64,64]{1,0:T(8,128)} %get-tuple-element.167) | copy-start | bytes 49156
  49.7 1.5 copy-start.28
  49.8 1.5 copy-start.29
  52.9 1.5 copy-start.26
  52.9 1.5 copy-start.27
  55.2 1.5 copy-start.24
  55.2 1.5 copy-start.25
  64.1 10.3 %copy-start.11 = (f32[8,8,2,32]{3,1,2,0:T(8,128)S(1)}, f32[8,8,2,32]{3,1,2,0:T(8,128)}, u32[]{:S(2)}) copy-start(f32[8,8,2,32]{3,1,2,0:T(8,128)} %copy.266) | copy-start | bytes 49156
  64.1 10.3 %copy-start.13 = (f32[8,8,2,32]{3,1,2,0:T(8,128)S(1)}, f32[8,8,2,32]{3,1,2,0:T(8,128)}, u32[]{:S(2)}) copy-start(f32[8,8,2,32]{3,1,2,0:T(8,128)} %copy.306) | copy-start | bytes 49156
  68.4 8.4 %copy-start.12 = (f32[8,8,2,32]{3,1,2,0:T(8,128)S(1)}, f32[8,8,2,32]{3,1,2,0:T(8,128)}, u32[]{:S(2)}) copy-start(f32[8,8,2,32]{3,1,2,0:T(8,128)} %copy.308) | copy-start | bytes 49156
  68.4 8.4 %copy-start.15 = (f32[8,8,2,32]{3,1,2,0:T(8,128)S(1)}, f32[8,8,2,32]{3,1,2,0:T(8,128)}, u32[]{:S(2)}) copy-start(f32[8,8,2,32]{3,1,2,0:T(8,128)} %copy.310) | copy-start | bytes 49156
  71.6 7.1 %copy-start.14 = (f32[8,8,2,32]{3,1,2,0:T(8,128)S(1)}, f32[8,8,2,32]{3,1,2,0:T(8,128)}, u32[]{:S(2)}) copy-start(f32[8,8,2,32]{3,1,2,0:T(8,128)} %copy.312) | copy-start | bytes 49156
  74.4 4.4 %copy-start = (f32[16,1,8,8,2,32]{5,4,3,2,0,1:T(2,128)S(1)}, f32[16,1,8,8,2,32]{5,4,3,2,0,1:T(2,128)}, u32[]{:S(2)}) copy-start(f32[16,1,8,8,2,32]{5,4,3,2,0,1:T(2,128)} %squeeze.32) | copy-start | bytes 786436
  74.4 4.4 %copy-start.2 = (f32[16,1,8,8,2,32]{5,4,3,2,0,1:T(2,128)S(1)}, f32[16,1,8,8,2,32]{5,4,3,2,0,1:T(2,128)}, u32[]{:S(2)}) copy-start(f32[16,1,8,8,2,32]{5,4,3,2,0,1:T(2,128)} %squeeze.33) | copy-start | bytes 786436
  74.4 6.1 %copy-start.1 = (f32[16,1,8,8,2,32]{5,4,3,2,0,1:T(2,128)S(1)}, f32[16,1,8,8,2,32]{5,4,3,2,0,1:T(2,128)}, u32[]{:S(2)}) copy-start(f32[16,1,8,8,2,32]{5,4,3,2,0,1:T(2,128)} %squeeze.35) | copy-start | bytes 786436
  74.4 6.1 %copy-start.16 = (f32[8,8,2,32]{3,1,2,0:T(8,128)S(1)}, f32[8,8,2,32]{3,1,2,0:T(8,128)}, u32[]{:S(2)}) copy-start(f32[8,8,2,32]{3,1,2,0:T(8,128)} %copy.316) | copy-start | bytes 49156
  74.4 6.1 %copy-start.17 = (f32[8,8,2,32]{3,1,2,0:T(8,128)S(1)}, f32[8,8,2,32]{3,1,2,0:T(8,128)}, u32[]{:S(2)}) copy-start(f32[8,8,2,32]{3,1,2,0:T(8,128)} %copy.318) | copy-start | bytes 49156
where the time goes:
time: 177 us; the launch traced here: 175 us
  Pallas kernels  65.1 us (37%)
  local copies, waits for them, and re-layouts  41.4 us (23%)
  other arithmetic  40.9 us (23%)
  matrix products  13.7 us (8%)
  starting transfers between devices  9.08 us (5%)
  between operations  4.52 us (3%)
    pallas_call x1, Pallas kernels, scatter_gather(): pl.pallas_call(lambda *refs: scatter_kernel(stages, *refs), out_shape=jax...  40 us
    pallas_call x1, Pallas kernels, gram_sum(): pl.pallas_call(lambda *refs: gram_sum_kernel(stages, *refs), out_shape=ja...  25.1 us
    squeeze x3, local copies, waits for them, and re-layouts, complex_times(): second[..., 0, :, :]  7 us
    mul x4, other arithmetic, shards(): born_scale[:, None, None, None]  6.83 us
    another operation x3, other arithmetic, shards(): lower_factor = jnp.linalg.cholesky(gram_matrix)  6.52 us
    dot_general x20, matrix products, transform(): jnp.einsum('nscb,sbtd->ntdc', turned, matrix, preferred_element_type=jnp....  6.05 us
    dot_general x20, matrix products, transform(): jnp.einsum('nrab,rasc->nscb', grid_values, matrix, preferred_element_type...  5.69 us
    squeeze x3, local copies, waits for them, and re-layouts, complex_times(): second[..., 1, :, :]  4.9 us
  transfers between devices with their start and end apart: 2, of which 0 were waited for; matrix products, arithmetic and copies ran while one was open for 14% of the time, Pallas kernels for 0%

commit v1 on v0

--- a/solution.py
+++ b/solution.py
@@ -99,79 +99,6 @@
         jnp.float32
     )
     return jnp.sum(onehot_rows * wavenum[None, :], axis=1)
-
-
-def gram_sum_kernel(stages, part_ref, out_ref, *scratch):
-    count = len(stages)
-    slots = scratch[:count]
-    send_sems, recv_sems, carried = scratch[count], scratch[count + 1], scratch[count + 2]
-    barrier = pltpu.get_barrier_semaphore()
-    peers_total = 0
-    for axis, size in stages:
-        me = lax.axis_index(axis)
-        for step in range(1, size):
-            pl.semaphore_signal(barrier, inc=1, device_id={axis: lax.rem(me + step, size)},
-                                device_id_type=pl.DeviceIdType.MESH)
-            peers_total += 1
-    pl.semaphore_wait(barrier, peers_total)
-    carried[...] = part_ref[...]
-    used = 0
-    offset = 0
-    for stage, (axis, size) in enumerate(stages):
-        me = lax.axis_index(axis)
-        slot = slots[stage]
-        copies = []
-        for step in range(1, size):
-            copy = pltpu.make_async_remote_copy(
-                src_ref=carried,
-                dst_ref=slot.at[me],
-                send_sem=send_sems.at[used + step - 1],
-                recv_sem=recv_sems.at[offset + me],
-                device_id={axis: lax.rem(me + step, size)},
-                device_id_type=pl.DeviceIdType.MESH,
-            )
-            copy.start()
-            copies.append(copy)
-        slot[me] = carried[...]
-        for copy in copies:
-            copy.wait_send()
-        for step in range(1, size):
-            sender = lax.rem(me + size - step, size)
-            incoming = pltpu.make_async_remote_copy(
-                src_ref=carried,
-                dst_ref=slot.at[sender],
-                send_sem=send_sems.at[used + step - 1],
-                recv_sem=recv_sems.at[offset + sender],
-                device_id={axis: lax.rem(me + step, size)},
-                device_id_type=pl.DeviceIdType.MESH,
-            )
-            incoming.wait_recv()
-        used += size - 1
-        offset += size
-        total = slot[0]
-        for member in range(1, size):
-            total = total + slot[member]
-        carried[...] = total
-    out_ref[...] = carried[...]
-
-
-def gram_sum(part, stages):
-    stages = [(axis, size) for axis, size in stages if size > 1]
-    sends = sum(size - 1 for _, size in stages)
-    scratch = [pltpu.VMEM((size,) + part.shape, jnp.float32) for _, size in stages]
-    scratch += [
-        pltpu.SemaphoreType.DMA((max(sends, 1),)),
-        pltpu.SemaphoreType.DMA((max(sum(size for _, size in stages), 1),)),
-        pltpu.VMEM(part.shape, jnp.float32),
-    ]
-    return pl.pallas_call(
-        lambda *refs: gram_sum_kernel(stages, *refs),
-        out_shape=jax.ShapeDtypeStruct(part.shape, jnp.float32),
-        in_specs=[pl.BlockSpec(memory_space=pltpu.VMEM)],
-        out_specs=pl.BlockSpec(memory_space=pltpu.VMEM),
-        scratch_shapes=scratch,
-        compiler_params=pltpu.CompilerParams(collective_id=0, has_side_effects=True),
-    )(part)
 
 
 def exchange(axis, size, current, slot, send_sems, recv_sems, offset, whole=False):
@@ -205,14 +132,16 @@
     return me
 
 
-def scatter_kernel(stages, part_ref, extra_ref, out_ref, *scratch):
+def reduce_kernel(stages, depth_size, divisor, row_total, part_ref, probe_ref, sketch_ref, gram_ref,
+                  *scratch):
     count = len(stages)
     slots = scratch[:count]
     sums = scratch[count : 2 * count - 1]
-    mine, gathered, send_sems, recv_sems = scratch[2 * count - 1 :]
+    gram_slots = scratch[2 * count - 1 : 3 * count - 1]
+    mine, gathered, carried, send_sems, recv_sems = scratch[3 * count - 1 :]
     barrier = pltpu.get_barrier_semaphore()
     peers_total = 0
-    for axis, size in stages + [("depth", out_ref.shape[0])]:
+    for axis, size in stages + [("depth", depth_size)]:
         me = lax.axis_index(axis)
         for step in range(1, size):
             pl.semaphore_signal(barrier, inc=1, device_id={axis: lax.rem(me + step, size)},
@@ -231,34 +160,55 @@
             sums[stage][...] = total
             current = sums[stage]
         else:
-            mine[0] = total
-    mine[1] = extra_ref[...]
-    depth_size = out_ref.shape[0]
+            mine[...] = total
     me = exchange("depth", depth_size, mine, gathered, send_sems, recv_sems, offset, whole=True)
+    offset += depth_size
     gathered[me] = mine[...]
-    out_ref[...] = gathered[...]
-
-
-def scatter_gather(part, extra, stages, depth_size):
+    summed = gathered[...].reshape(sketch_ref.shape)
+    sketch = summed / divisor + DAMPING * probe_ref[...]
+    sketch_ref[...] = sketch
+    carried[...] = lax.dot_general(
+        sketch, sketch, (((1,), (1,)), ((), ())), precision=lax.Precision.HIGHEST,
+        preferred_element_type=jnp.float32,
+    ) / row_total
+    for stage, (axis, size) in enumerate(stages):
+        slot = gram_slots[stage]
+        me = exchange(axis, size, carried, slot, send_sems, recv_sems, offset, whole=True)
+        offset += size
+        slot[me] = carried[...]
+        total = slot[0]
+        for member in range(1, size):
+            total = total + slot[member]
+        carried[...] = total
+    gram_ref[...] = carried[...]
+
+
+def reduce_all(part, probe_all, stages, depth_size, divisor, row_total):
     stages = [(axis, size) for axis, size in stages if size > 1]
     part = part.reshape(tuple(size for _, size in stages) + part.shape[-2:])
+    rows, width = probe_all.shape
     scratch = [pltpu.VMEM(part.shape[stage:], jnp.float32) for stage in range(len(stages))]
     scratch += [pltpu.VMEM(part.shape[stage + 1 :], jnp.float32) for stage in range(len(stages) - 1)]
-    block = (2,) + extra.shape
+    scratch += [pltpu.VMEM((size, rows, rows), jnp.float32) for _, size in stages]
+    semaphores = 2 * sum(size for _, size in stages) + depth_size
     scratch += [
-        pltpu.VMEM(block, jnp.float32),
-        pltpu.VMEM((depth_size,) + block, jnp.float32),
-        pltpu.SemaphoreType.DMA((sum(size for _, size in stages) + depth_size,)),
-        pltpu.SemaphoreType.DMA((sum(size for _, size in stages) + depth_size,)),
+        pltpu.VMEM(part.shape[-2:], jnp.float32),
+        pltpu.VMEM((depth_size,) + part.shape[-2:], jnp.float32),
+        pltpu.VMEM((rows, rows), jnp.float32),
+        pltpu.SemaphoreType.DMA((semaphores,)),
+        pltpu.SemaphoreType.DMA((semaphores,)),
     ]
     return pl.pallas_call(
-        lambda *refs: scatter_kernel(stages, *refs),
-        out_shape=jax.ShapeDtypeStruct((depth_size,) + block, jnp.float32),
+        lambda *refs: reduce_kernel(stages, depth_size, divisor, row_total, *refs),
+        out_shape=(
+            jax.ShapeDtypeStruct((rows, width), jnp.float32),
+            jax.ShapeDtypeStruct((rows, rows), jnp.float32),
+        ),
         in_specs=[pl.BlockSpec(memory_space=pltpu.VMEM)] * 2,
-        out_specs=pl.BlockSpec(memory_space=pltpu.VMEM),
+        out_specs=(pl.BlockSpec(memory_space=pltpu.VMEM), pl.BlockSpec(memory_space=pltpu.VMEM)),
         scratch_shapes=scratch,
-        compiler_params=pltpu.CompilerParams(collective_id=1, has_side_effects=True),
-    )(part, extra)
+        compiler_params=pltpu.CompilerParams(collective_id=2, has_side_effects=True),
+    )(part, probe_all)
 
 
 def shards(incident, encode, freq_index, wavenum, slowness, probes):
@@ -274,6 +224,14 @@
     plane_count = slowness_all.shape[0]
     probe_mine = lax.all_to_all(probes, "depth", 0, 1, tiled=True).astype(jnp.float32)
     probe_mine = probe_mine.reshape(probe_mine.shape[:2] + (SIDE, SIDE))
+    slab_points = probes.shape[2] // src_count
+    probe_slab = lax.dynamic_slice_in_dim(
+        probes, lax.axis_index(SRC_AXES) * slab_points, slab_points, 2
+    )
+    probe_slab = jnp.broadcast_to(probe_slab[None], (depth_count,) + probe_slab.shape)
+    probe_slab = lax.all_to_all(probe_slab, "depth", 0, 0, tiled=True)
+    probe_all = jnp.transpose(probe_slab[:, :, 0], (1, 0, 2)).reshape(probe_count, -1)
+    probe_all = probe_all.astype(jnp.float32)
     sources = encoded_sources(incident, encode, incident.shape[1])
     sources = sources.reshape(sources.shape[:-1] + (SIDE, SIDE))
     wave_nums = lookup_waves(freq_index, wavenum, wavenum.shape[0])
@@ -320,25 +278,14 @@
     by_axes = jnp.transpose(by_axes, (4, 3, 2, 0, 1, 5)).reshape(
         CORES, CHIPS_Z, CHIPS_Y, rows, planes * slab_width
     )
-    src_index = lax.axis_index(SRC_AXES)
-    probe_slab = lax.dynamic_slice_in_dim(probes, src_index * slab_width, slab_width, 2)
-    probe_slab = jnp.transpose(probe_slab.reshape(depth_count, rows, slab_width), (1, 0, 2))
-    probe_slab = probe_slab.reshape(rows, depth_count * slab_width).astype(jnp.float32)
     stage_sizes = [("core", CORES), ("chip_z", CHIPS_Z), ("chip_y", CHIPS_Y)]
-    both = scatter_gather(by_axes, probe_slab, stage_sizes, depth_count)
-    summed = both[:, 0].reshape(probe_count, planes, slab_width)
-    local_probes = jnp.transpose(
-        both[:, 1].reshape(depth_count, rows, depth_count, slab_width), (2, 1, 0, 3)
-    ).reshape(probe_count, planes, slab_width)
-    sketch_all = summed / (group_count * src_count) + DAMPING * local_probes
-    flattened_all = sketch_all.reshape(probe_count, -1)
-    row_total = flattened_all.shape[1] * src_count
-    gram_local = jnp.dot(flattened_all, flattened_all.T, precision=lax.Precision.HIGHEST) / row_total
-    stage_sizes = [(axis, lax.axis_size(axis)) for axis in ("core", "chip_z", "chip_y")]
-    gram_matrix = gram_sum(gram_local, stage_sizes)
-    sketch = lax.dynamic_slice_in_dim(sketch_all, lax.axis_index("depth"), 1, 1)
+    row_total = planes * slab_width * src_count
+    sketch_all, gram_matrix = reduce_all(
+        by_axes, probe_all, stage_sizes, depth_count, group_count * src_count, row_total
+    )
+    depth_index = lax.axis_index("depth")
+    flattened = lax.dynamic_slice_in_dim(sketch_all, depth_index * slab_width, slab_width, 1)
     local_planes = 1
-    flattened = sketch.reshape(probe_count, local_planes * slab_width)
     lower_factor = jnp.linalg.cholesky(gram_matrix)
     identity = jnp.eye(probe_count, dtype=jnp.float32)
     inverse_lower = lax.linalg.triangular_solve(lower_factor, identity, left_side=True, lower=True)

time: 177 us -> 175 us (0.989)
  Pallas kernels: 65.1 us -> 60 us
  waiting for transfers between devices: 0.01 us -> 3.69 us
  starting transfers between devices: 9.08 us -> 12.5 us
  other arithmetic: 40.9 us -> 38.8 us
    pallas_call x2 -> x1, Pallas kernels: 65.1 us -> 60 us  [reduce_all(): pl.pallas_call(lambda *refs: reduce_kernel(stages, depth_size, divisor, r...]
    all_to_all x0 -> x1, starting transfers between devices: none -> 4.84 us  [shards(): probe_slab = lax.all_to_all(probe_slab, 'depth', 0, 0, tiled=True)]
    all_to_all x1, waiting for transfers between devices: 0.01 us -> 3.68 us  [shards(): lax.all_to_all(spread, 'depth', 0, 0, tiled=True)]
    unnamed x65 -> x71, local copies, waits for them, and re-layouts: 3.24 us -> 4.17 us
  transfers between devices with their start and end apart: 2 -> 3, of which waited for: 0 -> 1; matrix products, arithmetic and copies ran while one was open for 14% -> 14% of each run, Pallas kernels for 0% -> 0%
where the time goes in v1:
time: 175 us; the launch traced here: 174 us
  Pallas kernels  60 us (34%)
  local copies, waits for them, and re-layouts  41 us (23%)
  other arithmetic  38.8 us (22%)
  matrix products  13.6 us (8%)
  starting transfers between devices  12.5 us (7%)
  between operations  4.34 us (2%)
  waiting for transfers between devices  3.69 us (2%)
    pallas_call x1, Pallas kernels, reduce_all(): pl.pallas_call(lambda *refs: reduce_kernel(stages, depth_size, divisor, r...  60 us
    squeeze x3, local copies, waits for them, and re-layouts, complex_times(): second[..., 0, :, :]  6.95 us
    mul x4, other arithmetic, shards(): born_scale[:, None, None, None]  6.6 us
    another operation x3, other arithmetic, shards(): lower_factor = jnp.linalg.cholesky(gram_matrix)  6.52 us
    dot_general x20, matrix products, transform(): jnp.einsum('nscb,sbtd->ntdc', turned, matrix, preferred_element_type=jnp....  6.06 us
    dot_general x20, matrix products, transform(): jnp.einsum('nrab,rasc->nscb', grid_values, matrix, preferred_element_type...  5.69 us
    squeeze x3, local copies, waits for them, and re-layouts, complex_times(): second[..., 1, :, :]  4.9 us
    another operation x1, other arithmetic, shards(): lax.linalg.triangular_solve(lower_factor, identity, left_side=True, lower...  4.9 us
  transfers between devices with their start and end apart: 3, of which 1 were waited for; matrix products, arithmetic and copies ran while one was open for 14% of the time, Pallas kernels for 0%

profile of v1, /device:TPU:1, one launch (start us, length us, event | category | flops | bytes accessed | tf_op | source)
XLA Modules:
  0.0 174.0 jit_solution(14768938606657989235)
XLA Ops:
  0.6 0.8 constant_dynamic-slice_fusion
  1.5 0.7 reshape.1992
  2.3 4.8 %all-to-all-start.2 = ((bf16[4,2,1024]{2,1,0:T(2,128)(2,1)}), bf16[4,2,1024]{2,1,0:T(2,128)(2,1)S(1)}, u32[]{:S(2)}, u32[]{:S(2)}) async-start(bf16[4,2,1024]{2,1,0:T(2,128)(2,1)} %reshape.1992), calls=%async_computation.2 | async-start | bytes 32768 | tf_op jit(solution)/shard_map/all_to_all | solution.py:232
  8.4 1.2 fusion.189
  11.7 1.0 multiply_reduce_fusion
  14.8 2.0 %reduce.13 = bf16[64,4096]{1,0:T(8,128)(2,1)S(1)} reduce(bf16[64,1,4096]{2,0,1:T(8,128)(2,1)} %param.11, bf16[]{:T(256)} %broadcast.1741), dimensions={1}, to_apply=%copy.308.reduce_sub_computation | reduce | bytes 1048578 | tf_op args[5]
  16.8 1.2 reshape.1990
  18.0 0.7 broadcast_in_dim.18
  18.7 4.2 %all-to-all-start = ((f32[4,1,4096]{2,1,0:T(1,128)}), f32[4,1,4096]{2,1,0:T(1,128)S(1)}, u32[]{:S(2)}, u32[]{:S(2)}) async-start(f32[4,1,4096]{2,1,0:T(1,128)} %broadcast_in_dim.18), calls=%async_computation | async-start | bytes 131072 | tf_op jit(solution)/shard_map/all_to_all | solution.py:223
  23.0 0.7 copy.363.refs_1_
  23.7 3.7 %all-to-all-done = f32[4,1,4096]{2,1,0:T(1,128)S(1)} async-done(((f32[4,1,4096]{2,1,0:T(1,128)}), f32[4,1,4096]{2,1,0:T(1,128)S(1)}, u32[]{:S(2)}, u32[]{:S(2)}) %all-to-all-start) | async-done | bytes 65568 | tf_op jit(solution)/shard_map/all_to_all | solution.py:223
  27.4 3.5 %all-to-all-start.1 = ((bf16[4,2,32768]{2,1,0:T(2,128)(2,1)}), bf16[4,2,32768]{2,1,0:T(2,128)(2,1)S(1)}, u32[]{:S(2)}, u32[]{:S(2)}) async-start(bf16[4,2,32768]{2,1,0:T(2,128)(2,1)} %reshape.1990), calls=%async_computation.1 | async-start | bytes 1048576 | tf_op jit(solution)/shard_map/all_to_all | solution.py:225
  30.9 2.8 %sine_reduce_fusion = (f32[4,4096]{1,0:T(4,128)S(1)}, f32[4,4096]{1,0:T(4,128)S(1)}) fusion(f32[4,1,4096]{2,1,0:T(1,128)S(1)} %all-to-all-done, f32[]{:T(128)} %fusion.189), kind=kLoop, calls=%fused_computation.237 | loop fusion | flops 16384 | bytes 196612 | tf_op jit(solution)/shard_map/sin | solution.py:87
  38.5 0.6 slice_bitcast_fusion.16
  39.2 0.6 copy.307
  39.9 0.6 copy.347
  40.7 0.6 copy.349
  43.6 0.6 copy.357
  44.3 0.6 copy.359
  45.6 0.7 slice_bitcast_fusion.9
  46.3 0.7 reshape.1991
  47.0 0.7 copy.585
  47.8 1.0 reshape.1890
  48.8 1.8 %multiply_bitcast_fusion = (f32[1,16,1,64,64]{4,3,1,2,0:T(8,128)S(1)}, f32[16,1,64,64]{3,2,1,0:T(8,128)S(1)}, f32[16,1,64,64]{3,2,1,0:T(8,128)S(1)}, bf16[16,1,6...) fusion(f32[16,4,64,64]{3,2,1,0:T(8,128)S(1)} %reshape.1890, ...), kind=kLoop, calls=%fused_computation.163 | loop fusion | flops 1048576 | bytes 2736132 | tf_op jit(solution)/shard_map/stack | solution.py:254
  58.1 1.2 fusion.68
  63.6 1.1 fusion.76
  67.7 1.6 squeeze.29
  69.3 1.6 squeeze.30
  71.0 2.7 %squeeze.31 = f32[16,1,8,8,2,32]{5,4,3,2,0,1:T(2,128)} reshape(f32[1,16,1,64,64]{4,3,1,2,0:T(8,128)} %get-tuple-element.90) | data formatting | bytes 524288 | tf_op jit(solution)/shard_map/squeeze | solution.py:59
  73.6 1.6 squeeze.32
  75.2 1.6 squeeze.33
  76.8 1.6 squeeze.34
  78.5 2.7 %squeeze.35 = f32[16,1,8,8,2,32]{5,4,3,2,0,1:T(2,128)} reshape(f32[1,16,1,64,64]{4,3,1,2,0:T(8,128)} %get-tuple-element.94) | data formatting | bytes 524288 | tf_op jit(solution)/shard_map/squeeze | solution.py:59
  81.2 2.3 %fusion.9 = f32[16,1,8,8,2,32]{5,3,4,2,1,0:T(8,128)S(1)} fusion(f32[16,1,8,8,2,32]{5,4,3,2,0,1:T(2,128)} %squeeze.29, f32[16,1,8,8,2,32]{5,4,3,2,0,1:T(2,128)S(1)} %squeeze.28, f32[8,8,2,32]{3,1,2,0:T(8,128)S(1)} %copy-done.13, f32[8,8,2,32]{3,1,2,0:T(8,128)S(1)} %copy-done.11, f32[]{:T(128)} %fusion.189), kind=kLoop, calls=%fused_computation.61 | loop fusion | flops 262144 | bytes 819204 | tf_op jit(solution)/shard_map/mul | solution.py:267
  83.6 1.9 %fusion.7 = f32[16,1,8,8,2,32]{5,3,4,2,1,0:T(8,128)S(1)} fusion(f32[16,1,8,8,2,32]{5,4,3,2,0,1:T(2,128)} %squeeze.31, f32[16,1,8,8,2,32]{5,4,3,2,0,1:T(2,128)S(1)} %squeeze.30, f32[8,8,2,32]{3,1,2,0:T(8,128)S(1)} %copy-done.15, f32[8,8,2,32]{3,1,2,0:T(8,128)S(1)} %copy-done.12, f32[]{:T(128)} %fusion.189), kind=kLoop, calls=%fused_computation.57 | loop fusion | flops 262144 | bytes 819204 | tf_op jit(solution)/shard_map/mul | solution.py:267
  85.5 1.6 fusion.5
  87.1 0.8 fusion.3
  88.5 4.7 %copy.361 = f32[2,8,8,16,4,32]{5,4,3,2,1,0:T(4,128)} copy(f32[2,8,8,16,4,32]{5,1,0,2,4,3:T(8,128)S(1)} %maximum_bitcast_fusion) | data formatting | bytes 2097152 | tf_op jit(solution)/shard_map/transpose | solution.py:278
  93.1 4.5 %reshape.1888.refs_0_ = f32[2,8,8,16,128]{4,3,2,1,0:T(8,128)} reshape(f32[2,8,8,16,4,32]{5,4,3,2,1,0:T(4,128)} %copy.361) | data formatting | bytes 2097152 | tf_op jit(solution)/shard_map/reshape | solution.py:278
  97.7 60.0 %shard_map.77 = (f32[64,128]{1,0:T(8,128)}, f32[64,64]{1,0:T(8,128)}) custom-call(f32[2,8,8,16,128]{4,3,2,1,0:T(8,128)} %reshape.1888.refs_0_, f32[64,128]{1,0:T(8,128)} %copy.363.refs_1_), custom_call_target="tpu_custom_call" | custom-call | tf_op jit(solution)/shard_map/pallas_call | solution.py:201
  157.7 0.8 copy.364
  158.5 0.8 fusion.145
  159.3 5.8 %cholesky.16 = f32[64,64]{1,0:T(8,128)S(1)} custom-call(f32[64,64]{1,0:T(8,128)S(1)} %fusion.145), custom_call_target="Cholesky" | custom-call | tf_op jit(solution)/shard_map/jit(cholesky)/cholesky | solution.py:289
  165.2 0.6 compare_reduce_fusion
  165.8 0.7 fusion.158
  166.5 4.9 %custom-call.6 = f32[1,64,64]{1,2,0:T(8,128)S(1)} custom-call(f32[1,64,64]{2,1,0:T(8,128)S(1)} %get-tuple-element.152), custom_call_target="InvertDiagBlocksLowerTriangular" | custom-call | tf_op jit(solution)/shard_map/triangular_solve | solution.py:291
  171.6 0.7 copy.365
  172.3 1.7 convolution_bitcast_fusion.40
  (187 shorter events, 26.0 us)
Async XLA Ops:
  0.6 17.4 %copy-start.30 = (f32[1,4096]{1,0:T(1,128)S(1)}, f32[1,4096]{1,0:T(1,128)}, u32[]{:S(2)}) copy-start(f32[1,4096]{1,0:T(1,128)} %param.10) | copy-start | bytes 49156
  2.3 15.8 %all-to-all-start.2 = ((bf16[4,2,1024]{2,1,0:T(2,128)(2,1)}), bf16[4,2,1024]{2,1,0:T(2,128)(2,1)S(1)}, u32[]{:S(2)}, u32[]{:S(2)}) async-start(bf16[4,2,1024]{2,1,0:T(2,128)(2,1)} %reshape.1992), calls=%async_computation.2 | async-start | bytes 32768 | tf_op jit(solution)/shard_map/all_to_all | solution.py:232
  18.7 8.7 %all-to-all-start = ((f32[4,1,4096]{2,1,0:T(1,128)}), f32[4,1,4096]{2,1,0:T(1,128)S(1)}, u32[]{:S(2)}, u32[]{:S(2)}) async-start(f32[4,1,4096]{2,1,0:T(1,128)} %broadcast_in_dim.18), calls=%async_computation | async-start | bytes 131072 | tf_op jit(solution)/shard_map/all_to_all | solution.py:223
  27.4 18.9 %all-to-all-start.1 = ((bf16[4,2,32768]{2,1,0:T(2,128)(2,1)}), bf16[4,2,32768]{2,1,0:T(2,128)(2,1)S(1)}, u32[]{:S(2)}, u32[]{:S(2)}) async-start(bf16[4,2,32768]{2,1,0:T(2,128)(2,1)} %reshape.1990), calls=%async_computation.1 | async-start | bytes 1048576 | tf_op jit(solution)/shard_map/all_to_all | solution.py:225
  34.0 12.3 %copy-start.3 = (f32[1,1,64,64]{3,2,1,0:T(8,128)}, f32[1,1,64,64]{3,2,1,0:T(8,128)S(1)}, u32[]{:S(2)}) copy-start(f32[1,1,64,64]{3,2,1,0:T(8,128)S(1)} %get-tuple-element.112) | copy-start | bytes 49156
  35.3 11.0 %copy-start.4 = (f32[1,1,64,64]{3,2,1,0:T(8,128)}, f32[1,1,64,64]{3,2,1,0:T(8,128)S(1)}, u32[]{:S(2)}) copy-start(f32[1,1,64,64]{3,2,1,0:T(8,128)S(1)} %get-tuple-element.25) | copy-start | bytes 49156
  35.3 11.0 %copy-start.5 = (f32[1,1,64,64]{3,2,1,0:T(8,128)}, f32[1,1,64,64]{3,2,1,0:T(8,128)S(1)}, u32[]{:S(2)}) copy-start(f32[1,1,64,64]{3,2,1,0:T(8,128)S(1)} %get-tuple-element.110) | copy-start | bytes 49156
  36.5 9.7 %copy-start.6 = (f32[1,1,64,64]{3,2,1,0:T(8,128)}, f32[1,1,64,64]{3,2,1,0:T(8,128)S(1)}, u32[]{:S(2)}) copy-start(f32[1,1,64,64]{3,2,1,0:T(8,128)S(1)} %get-tuple-element.23) | copy-start | bytes 49156
  36.6 9.7 %copy-start.7 = (f32[1,1,64,64]{3,2,1,0:T(8,128)}, f32[1,1,64,64]{3,2,1,0:T(8,128)S(1)}, u32[]{:S(2)}) copy-start(f32[1,1,64,64]{3,2,1,0:T(8,128)S(1)} %get-tuple-element.108) | copy-start | bytes 49156
  37.8 8.5 %copy-start.8 = (f32[1,1,64,64]{3,2,1,0:T(8,128)}, f32[1,1,64,64]{3,2,1,0:T(8,128)S(1)}, u32[]{:S(2)}) copy-start(f32[1,1,64,64]{3,2,1,0:T(8,128)S(1)} %get-tuple-element.100) | copy-start | bytes 49156
  37.8 8.5 %copy-start.9 = (f32[1,1,64,64]{3,2,1,0:T(8,128)}, f32[1,1,64,64]{3,2,1,0:T(8,128)S(1)}, u32[]{:S(2)}) copy-start(f32[1,1,64,64]{3,2,1,0:T(8,128)S(1)} %get-tuple-element.99) | copy-start | bytes 49156
  51.1 1.5 copy-start.22
  51.1 1.5 copy-start.23
  53.3 1.5 copy-start.20
  53.4 1.5 copy-start.21
  55.4 1.3 copy-start.10
  56.0 1.7 %copy-start.18 = (f32[64,64]{1,0:T(8,128)S(1)}, f32[64,64]{1,0:T(8,128)}, u32[]{:S(2)}) copy-start(f32[64,64]{1,0:T(8,128)} %get-tuple-element.104) | copy-start | bytes 49156
  56.0 1.7 %copy-start.19 = (f32[64,64]{1,0:T(8,128)S(1)}, f32[64,64]{1,0:T(8,128)}, u32[]{:S(2)}) copy-start(f32[64,64]{1,0:T(8,128)} %get-tuple-element.169) | copy-start | bytes 49156
  56.7 1.4 copy-start.28
  56.7 1.4 copy-start.29
  59.8 1.5 copy-start.26
  59.8 1.5 copy-start.27
  62.1 1.5 copy-start.24
  62.1 1.5 copy-start.25
  70.9 10.2 %copy-start.11 = (f32[8,8,2,32]{3,1,2,0:T(8,128)S(1)}, f32[8,8,2,32]{3,1,2,0:T(8,128)}, u32[]{:S(2)}) copy-start(f32[8,8,2,32]{3,1,2,0:T(8,128)} %copy.307) | copy-start | bytes 49156
  70.9 10.2 %copy-start.13 = (f32[8,8,2,32]{3,1,2,0:T(8,128)S(1)}, f32[8,8,2,32]{3,1,2,0:T(8,128)}, u32[]{:S(2)}) copy-start(f32[8,8,2,32]{3,1,2,0:T(8,128)} %copy.347) | copy-start | bytes 49156
  75.2 8.3 %copy-start.12 = (f32[8,8,2,32]{3,1,2,0:T(8,128)S(1)}, f32[8,8,2,32]{3,1,2,0:T(8,128)}, u32[]{:S(2)}) copy-start(f32[8,8,2,32]{3,1,2,0:T(8,128)} %copy.349) | copy-start | bytes 49156
  75.2 8.4 %copy-start.15 = (f32[8,8,2,32]{3,1,2,0:T(8,128)S(1)}, f32[8,8,2,32]{3,1,2,0:T(8,128)}, u32[]{:S(2)}) copy-start(f32[8,8,2,32]{3,1,2,0:T(8,128)} %copy.351) | copy-start | bytes 49156
  78.5 7.0 %copy-start.14 = (f32[8,8,2,32]{3,1,2,0:T(8,128)S(1)}, f32[8,8,2,32]{3,1,2,0:T(8,128)}, u32[]{:S(2)}) copy-start(f32[8,8,2,32]{3,1,2,0:T(8,128)} %copy.353) | copy-start | bytes 49156
  81.2 4.3 %copy-start = (f32[16,1,8,8,2,32]{5,4,3,2,0,1:T(2,128)S(1)}, f32[16,1,8,8,2,32]{5,4,3,2,0,1:T(2,128)}, u32[]{:S(2)}) copy-start(f32[16,1,8,8,2,32]{5,4,3,2,0,1:T(2,128)} %squeeze.32) | copy-start | bytes 786436
  81.2 4.3 %copy-start.2 = (f32[16,1,8,8,2,32]{5,4,3,2,0,1:T(2,128)S(1)}, f32[16,1,8,8,2,32]{5,4,3,2,0,1:T(2,128)}, u32[]{:S(2)}) copy-start(f32[16,1,8,8,2,32]{5,4,3,2,0,1:T(2,128)} %squeeze.33) | copy-start | bytes 786436
  81.2 5.9 %copy-start.1 = (f32[16,1,8,8,2,32]{5,4,3,2,0,1:T(2,128)S(1)}, f32[16,1,8,8,2,32]{5,4,3,2,0,1:T(2,128)}, u32[]{:S(2)}) copy-start(f32[16,1,8,8,2,32]{5,4,3,2,0,1:T(2,128)} %squeeze.35) | copy-start | bytes 786436
  81.2 5.9 %copy-start.16 = (f32[8,8,2,32]{3,1,2,0:T(8,128)S(1)}, f32[8,8,2,32]{3,1,2,0:T(8,128)}, u32[]{:S(2)}) copy-start(f32[8,8,2,32]{3,1,2,0:T(8,128)} %copy.357) | copy-start | bytes 49156
  81.2 5.9 %copy-start.17 = (f32[8,8,2,32]{3,1,2,0:T(8,128)S(1)}, f32[8,8,2,32]{3,1,2,0:T(8,128)}, u32[]{:S(2)}) copy-start(f32[8,8,2,32]{3,1,2,0:T(8,128)} %copy.359) | copy-start | bytes 49156

commit v2 on v1

--- a/solution.py
+++ b/solution.py
@@ -219,19 +219,32 @@
     probe_count = probes.shape[0]
     src_count = lax.axis_size(SRC_AXES)
     depth_count = lax.axis_size("depth")
-    spread = jnp.broadcast_to(slowness[None], (depth_count,) + slowness.shape)
-    slowness_all = lax.all_to_all(spread, "depth", 0, 0, tiled=True).reshape(-1, slowness.shape[-1])
-    plane_count = slowness_all.shape[0]
-    probe_mine = lax.all_to_all(probes, "depth", 0, 1, tiled=True).astype(jnp.float32)
-    probe_mine = probe_mine.reshape(probe_mine.shape[:2] + (SIDE, SIDE))
-    slab_points = probes.shape[2] // src_count
+    rows = probe_count // depth_count
+    points = probes.shape[2]
+    slab_points = points // src_count
     probe_slab = lax.dynamic_slice_in_dim(
         probes, lax.axis_index(SRC_AXES) * slab_points, slab_points, 2
     )
-    probe_slab = jnp.broadcast_to(probe_slab[None], (depth_count,) + probe_slab.shape)
-    probe_slab = lax.all_to_all(probe_slab, "depth", 0, 0, tiled=True)
-    probe_all = jnp.transpose(probe_slab[:, :, 0], (1, 0, 2)).reshape(probe_count, -1)
-    probe_all = probe_all.astype(jnp.float32)
+    high = slowness.astype(jnp.bfloat16)
+    rest = slowness - high.astype(jnp.float32)
+    middle = rest.astype(jnp.bfloat16)
+    low = (rest - middle.astype(jnp.float32)).astype(jnp.bfloat16)
+    shared = jnp.concatenate([probe_slab.reshape(-1), high.reshape(-1), middle.reshape(-1), low.reshape(-1)])
+    payload = jnp.concatenate(
+        [probes.reshape(depth_count, -1), jnp.broadcast_to(shared[None], (depth_count,) + shared.shape)],
+        axis=1,
+    )
+    payload = lax.all_to_all(payload, "depth", 0, 0, tiled=True)
+    cut = rows * points
+    probe_mine = jnp.transpose(payload[:, :cut].reshape(depth_count, rows, points), (1, 0, 2))
+    probe_mine = probe_mine.astype(jnp.float32)
+    probe_mine = probe_mine.reshape(probe_mine.shape[:2] + (SIDE, SIDE))
+    slab_size = probe_count * slab_points
+    probe_all = payload[:, cut : cut + slab_size].reshape(depth_count, probe_count, slab_points)
+    probe_all = jnp.transpose(probe_all, (1, 0, 2)).reshape(probe_count, -1).astype(jnp.float32)
+    parts = payload[:, cut + slab_size :].reshape(depth_count, 3, points).astype(jnp.float32)
+    slowness_all = (parts[:, 0] + parts[:, 1]) + parts[:, 2]
+    plane_count = slowness_all.shape[0]
     sources = encoded_sources(incident, encode, incident.shape[1])
     sources = sources.reshape(sources.shape[:-1] + (SIDE, SIDE))
     wave_nums = lookup_waves(freq_index, wavenum, wavenum.shape[0])
@@ -271,7 +284,7 @@
         if plane > 0:
             turned_back = complex_times(conjugate(plane_screens[:, plane])[:, None], adjoint)
             adjoint = propagate(turned_back, spectra_back[:, None], forward, inverse)
-    sketch_part = jnp.stack(pieces, axis=1)
+    sketch_part = lax.optimization_barrier(jnp.stack(pieces, axis=1))
     rows, planes = sketch_part.shape[0], sketch_part.shape[1]
     by_axes = sketch_part.reshape(rows, planes, CHIPS_Y, CHIPS_Z, CORES, -1)
     slab_width = by_axes.shape[-1]
@@ -287,11 +300,9 @@
     flattened = lax.dynamic_slice_in_dim(sketch_all, depth_index * slab_width, slab_width, 1)
     local_planes = 1
     lower_factor = jnp.linalg.cholesky(gram_matrix)
-    identity = jnp.eye(probe_count, dtype=jnp.float32)
-    inverse_lower = lax.linalg.triangular_solve(lower_factor, identity, left_side=True, lower=True)
-    sketch_basis = jnp.dot(inverse_lower, flattened, precision=lax.Precision.HIGHEST).reshape(
-        probe_count, local_planes, slab_width
-    )
+    sketch_basis = lax.linalg.triangular_solve(
+        lower_factor, flattened, left_side=True, lower=True
+    ).reshape(probe_count, local_planes, slab_width)
     return (sketch_basis, lower_factor.T)
 
 

time: 175 us -> 147 us (0.84)
  local copies, waits for them, and re-layouts: 41 us -> 28.4 us
  starting transfers between devices: 12.5 us -> 4.84 us
  other arithmetic: 38.8 us -> 33.6 us
  waiting for transfers between devices: 3.69 us -> 1.75 us
    squeeze x8 -> x0, local copies, waits for them, and re-layouts: 14.1 us -> none  [the longest x3 6.95 us: complex_times(): second[..., 0, :, :]]
    reshape x0 -> x5, local copies, waits for them, and re-layouts: none -> 13 us  [the longest x2 10.6 us: shards(): by_axes = sketch_part.reshape(rows, planes, CHIPS_Y, CHIPS_Z, CORES, -1)]
    all_to_all x3 -> x1, starting transfers between devices: 12.5 us -> 4.84 us  [shards(): payload = lax.all_to_all(payload, 'depth', 0, 0, tiled=True)]
    mul x16 -> x0, local copies, waits for them, and re-layouts: 5.76 us -> none  [the longest x8 2.88 us: born(): -scaled * background[:, None, 1]]
    transpose x1 -> x0, local copies, waits for them, and re-layouts: 4.68 us -> none  [shards(): jnp.transpose(by_axes, (4, 3, 2, 0, 1, 5))]
    mul x4, other arithmetic: 6.6 us -> 2.75 us  [shards(): born_scale[:, None, None, None]]
    unnamed x1 -> x0, other arithmetic: 2.03 us -> none
    all_to_all x3 -> x1, waiting for transfers between devices: 3.69 us -> 1.75 us  [shards(): payload = lax.all_to_all(payload, 'depth', 0, 0, tiled=True)]
  transfers between devices with their start and end apart: 3 -> 1, of which waited for: 1 -> 1; matrix products, arithmetic and copies ran while one was open for 14% -> 2% of each run, Pallas kernels for 0% -> 0%
where the time goes in v2:
time: 147 us; the launch traced here: 146 us
  Pallas kernels  59.3 us (40%)
  other arithmetic  33.6 us (23%)
  local copies, waits for them, and re-layouts  28.4 us (19%)
  matrix products  13.7 us (9%)
  starting transfers between devices  4.84 us (3%)
  between operations  4.07 us (3%)
  waiting for transfers between devices  1.75 us (1%)
    pallas_call x1, Pallas kernels, reduce_all(): pl.pallas_call(lambda *refs: reduce_kernel(stages, depth_size, divisor, r...  59.3 us
    reshape x2, local copies, waits for them, and re-layouts, shards(): by_axes = sketch_part.reshape(rows, planes, CHIPS_Y, CHIPS_Z, CORES, -1)  10.6 us
    another operation x3, other arithmetic, shards(): lower_factor = jnp.linalg.cholesky(gram_matrix)  6.52 us
    dot_general x20, matrix products, transform(): jnp.einsum('nscb,sbtd->ntdc', turned, matrix, preferred_element_type=jnp....  6.28 us
    dot_general x20, matrix products, transform(): jnp.einsum('nrab,rasc->nscb', grid_values, matrix, preferred_element_type...  5.76 us
    another operation x1, other arithmetic, shards(): lax.linalg.triangular_solve(lower_factor, flattened, left_side=True, lowe...  4.89 us
    all_to_all x1, starting transfers between devices, shards(): payload = lax.all_to_all(payload, 'depth', 0, 0, tiled=True)  4.84 us
    reshape x1, local copies, waits for them, and re-layouts, shards(): jnp.transpose(by_axes, (4, 3, 2, 0, 1, 5))  4.53 us
  transfers between devices with their start and end apart: 1, of which 1 were waited for; matrix products, arithmetic and copies ran while one was open for 2% of the time, Pallas kernels for 0%

profile of v2, /device:TPU:1, one launch (start us, length us, event | category | flops | bytes accessed | tf_op | source)
XLA Modules:
  0.0 145.7 jit_solution(1838358768831293283)
XLA Ops:
  0.6 1.4 reshape.1906
  2.1 0.8 constant_dynamic-slice_fusion
  3.0 0.9 convert_reduce_fusion.2
  4.3 0.5 broadcast.1731
  4.8 1.5 %reduce.15 = bf16[4,79872]{1,0:T(4,128)(2,1)S(1)} reduce(bf16[4,1,79872]{2,0,1:T(4,128)(2,1)S(1)} %maximum_bitcast_fusion, bf16[]{:T(256)} %broadcast.1731), dimensions={1}, to_apply=%copy.229.reduce_sub_computation | reduce | bytes 1277954 | tf_op jit(solution)/shard_map/all_to_all | solution.py:237
  6.3 1.3 reshape.2035
  7.6 4.8 %all-to-all-start = ((bf16[4,2,39936]{2,1,0:T(2,128)(2,1)}), bf16[4,2,39936]{2,1,0:T(2,128)(2,1)S(1)}, u32[]{:S(2)}, u32[]{:S(2)}) async-start(bf16[4,2,39936]{2,1,0:T(2,128)(2,1)} %reshape.2035), calls=%async_computation | async-start | bytes 1277952 | tf_op jit(solution)/shard_map/all_to_all | solution.py:237
  13.5 0.6 fusion.192
  18.2 1.7 %all-to-all-done = bf16[4,2,39936]{2,1,0:T(2,128)(2,1)S(1)} async-done(((bf16[4,2,39936]{2,1,0:T(2,128)(2,1)}), bf16[4,2,39936]{2,1,0:T(2,128)(2,1)S(1)}, u32[]{:S(2)}, u32[]{:S(2)}) %all-to-all-start) | async-done | bytes 639008 | tf_op jit(solution)/shard_map/all_to_all | solution.py:237
  20.0 0.7 reshape.2036
  20.7 0.5 copy.481
  21.5 0.7 copy.278.refs_1_
  22.3 1.0 fusion.223
  23.5 0.4 cos.176
  24.0 0.7 slice_bitcast_fusion.11
  24.8 0.6 convert_bitcast_fusion.4
  26.6 0.7 convert_bitcast_fusion.2
  28.5 0.7 convert_bitcast_fusion
  30.4 0.7 add_bitcast_fusion.2
  31.1 0.6 slice_bitcast_fusion.17
  31.7 0.6 slice_bitcast_fusion.18
  32.3 0.6 slice_bitcast_fusion.19
  33.0 0.6 copy.480
  33.6 0.8 reshape.1930
  34.4 1.4 fusion.38
  35.9 1.9 %multiply_bitcast_fusion.1 = (f32[1,16,1,64,64]{4,3,1,2,0:T(8,128)S(1)}, f32[1,16,1,64,64]{4,3,1,2,0:T(8,128)S(1)}, f32[16,1,64,64]{3,2,0,1:T(8,128)S(1)}, f32[1...) fusion(f32[16,4,64,64]{3,2,0,1:T(8,128)S(1)} %reshape.1930, ...), kind=kLoop, calls=%fused_computation.174 | loop fusion | flops 1048576 | bytes 2867204 | tf_op jit(solution)/shard_map/stack | solution.py:267
  39.4 0.4 convolution_bitcast_fusion.20
  43.9 0.4 convolution_bitcast_fusion.12
  44.7 0.5 copy-done.4
  45.2 0.7 bitcast_multiply_fusion
  46.6 0.6 convolution_bitcast_fusion.10
  48.4 0.7 fusion.11
  49.8 0.4 convolution_bitcast_fusion.6
  51.3 0.7 fusion.14
  53.8 0.4 convolution_bitcast_fusion
  54.2 0.7 bitcast_multiply_fusion.1
  55.2 3.7 %reshape.1925 = f32[16,4,8,8,2,32]{5,4,3,2,1,0:T(2,128)} reshape(f32[16,4,64,64]{3,2,1,0:T(8,128)S(1)} %pad_maximum_fusion) | data formatting | bytes 2097152 | tf_op jit(solution)/shard_map/reshape | solution.py:289
  59.0 6.9 %copy.479 = f32[16,4,8,8,2,32]{5,1,0,2,3,4:T(4,128)} copy(f32[16,4,8,8,2,32]{5,4,3,2,1,0:T(2,128)} %reshape.1925) | data formatting | bytes 2097152 | tf_op jit(solution)/shard_map/reshape | solution.py:289
  65.8 4.5 %reshape.1926.refs_0_ = f32[2,8,8,16,128]{4,3,2,1,0:T(8,128)} reshape(f32[2,8,8,16,4,32]{5,4,3,2,1,0:T(4,128)} %bitcast.694) | data formatting | bytes 2097152 | tf_op jit(solution)/shard_map/reshape | solution.py:291
  70.3 59.3 %shard_map.77 = (f32[64,128]{1,0:T(8,128)}, f32[64,64]{1,0:T(8,128)}) custom-call(f32[2,8,8,16,128]{4,3,2,1,0:T(8,128)} %reshape.1926.refs_0_, f32[64,128]{1,0:T(8,128)} %copy.278.refs_1_), custom_call_target="tpu_custom_call" | custom-call | tf_op jit(solution)/shard_map/pallas_call | solution.py:201
  129.7 0.8 copy.279
  130.5 0.8 fusion.148
  131.3 5.8 %cholesky.15 = f32[64,64]{1,0:T(8,128)S(1)} custom-call(f32[64,64]{1,0:T(8,128)S(1)} %fusion.148), custom_call_target="Cholesky" | custom-call | tf_op jit(solution)/shard_map/jit(cholesky)/cholesky | solution.py:302
  137.2 0.6 compare_reduce_fusion
  137.8 0.7 fusion.161
  138.5 0.7 copy.280
  139.2 4.9 %custom-call.6 = f32[1,64,64]{1,2,0:T(8,128)S(1)} custom-call(f32[1,64,64]{2,1,0:T(8,128)S(1)} %get-tuple-element.145), custom_call_target="InvertDiagBlocksLowerTriangular" | custom-call | tf_op jit(solution)/shard_map/triangular_solve | solution.py:303
  144.1 1.7 %convolution_bitcast_fusion.40 = f32[64,1,32]{0,2,1:T(8,128)} fusion(f32[1,64,64]{1,2,0:T(8,128)S(1)} %custom-call.6, f32[64,128]{1,0:T(8,128)} %get-tuple-element.5, s32[]{:T(128)S(6)} %select_n.358), kind=kOutput, calls=%fused_computation.42 | convolution fusion | flops 1572864 | bytes 57348 | tf_op jit(solution)/shard_map/triangular_solve | solution.py:303
  (145 shorter events, 18.6 us)
Async XLA Ops:
  4.3 9.2 %copy-start.20 = (f32[8]{0:T(128)S(1)}, f32[8]{0:T(128)}, u32[]{:S(2)}) copy-start(f32[8]{0:T(128)} %param.9) | copy-start | bytes 100
  4.3 12.2 %copy-start.13 = (f32[1,4,2,4096]{3,2,1,0:T(2,128)S(1)}, f32[1,4,2,4096]{3,2,1,0:T(2,128)}, u32[]{:S(2)}) copy-start(f32[1,4,2,4096]{3,2,1,0:T(2,128)} %param.6) | copy-start | bytes 393220
  7.6 12.4 %all-to-all-start = ((bf16[4,2,39936]{2,1,0:T(2,128)(2,1)}), bf16[4,2,39936]{2,1,0:T(2,128)(2,1)S(1)}, u32[]{:S(2)}, u32[]{:S(2)}) async-start(bf16[4,2,39936]{2,1,0:T(2,128)(2,1)} %reshape.2035), calls=%async_computation | async-start | bytes 1277952 | tf_op jit(solution)/shard_map/all_to_all | solution.py:237
  38.8 1.0 copy-start.11
  38.9 1.0 copy-start.12
  41.1 0.9 copy-start.9
  41.1 0.9 copy-start.10
  43.3 1.0 copy-start.7
  43.3 1.0 copy-start.8
  44.4 0.8 copy-start.4
  44.5 0.8 copy-start.5
  44.5 1.5 copy-start.18
  44.5 1.5 copy-start.19
  47.4 1.0 copy-start.2
  47.4 1.0 copy-start.3
  47.8 1.3 copy-start.16
  47.8 1.3 copy-start.17
  50.3 1.0 copy-start
  50.3 1.0 copy-start.1
  50.7 1.3 copy-start.14
  50.7 1.3 copy-start.15
  53.3 0.9 copy-start.6

commit v3 on v2

--- a/solution.py
+++ b/solution.py
@@ -101,8 +101,25 @@
     return jnp.sum(onehot_rows * wavenum[None, :], axis=1)
 
 
-def exchange(axis, size, current, slot, send_sems, recv_sems, offset, whole=False):
-    me = lax.axis_index(axis)
+def member_of(group):
+    index = 0
+    total = 1
+    for axis, size in group:
+        index = index * size + lax.axis_index(axis)
+        total *= size
+    return index, total
+
+
+def device_of(group, index):
+    place = {}
+    for axis, size in reversed(group):
+        place[axis] = lax.rem(index, size)
+        index = index // size
+    return place
+
+
+def exchange(group, current, slot, send_sems, recv_sems, offset, whole=False):
+    me, size = member_of(group)
     copies = []
     for step in range(1, size):
         peer = lax.rem(me + step, size)
@@ -111,7 +128,7 @@
             dst_ref=slot.at[me],
             send_sem=send_sems.at[offset + peer],
             recv_sem=recv_sems.at[offset + me],
-            device_id={axis: peer},
+            device_id=device_of(group, peer),
             device_id_type=pl.DeviceIdType.MESH,
         )
         copy.start()
@@ -125,33 +142,34 @@
             dst_ref=slot.at[sender],
             send_sem=send_sems.at[offset + sender],
             recv_sem=recv_sems.at[offset + sender],
-            device_id={axis: sender},
+            device_id=device_of(group, sender),
             device_id_type=pl.DeviceIdType.MESH,
         )
         incoming.wait_recv()
     return me
 
 
-def reduce_kernel(stages, depth_size, divisor, row_total, part_ref, probe_ref, sketch_ref, gram_ref,
-                  *scratch):
+def reduce_kernel(stages, gram_groups, depth_size, divisor, row_total, part_ref, probe_ref, sketch_ref,
+                  gram_ref, *scratch):
     count = len(stages)
     slots = scratch[:count]
     sums = scratch[count : 2 * count - 1]
-    gram_slots = scratch[2 * count - 1 : 3 * count - 1]
-    mine, gathered, carried, send_sems, recv_sems = scratch[3 * count - 1 :]
+    groups = len(gram_groups)
+    gram_slots = scratch[2 * count - 1 : 2 * count - 1 + groups]
+    mine, gathered, carried, send_sems, recv_sems = scratch[2 * count - 1 + groups :]
     barrier = pltpu.get_barrier_semaphore()
     peers_total = 0
-    for axis, size in stages + [("depth", depth_size)]:
-        me = lax.axis_index(axis)
+    for group in gram_groups + [[("depth", depth_size)]]:
+        me, size = member_of(group)
         for step in range(1, size):
-            pl.semaphore_signal(barrier, inc=1, device_id={axis: lax.rem(me + step, size)},
+            pl.semaphore_signal(barrier, inc=1, device_id=device_of(group, lax.rem(me + step, size)),
                                 device_id_type=pl.DeviceIdType.MESH)
             peers_total += 1
     pl.semaphore_wait(barrier, peers_total)
     current = part_ref
     offset = 0
     for stage, (axis, size) in enumerate(stages):
-        me = exchange(axis, size, current, slots[stage], send_sems, recv_sems, offset)
+        me = exchange([(axis, size)], current, slots[stage], send_sems, recv_sems, offset)
         offset += size
         total = current[me]
         for step in range(1, size):
@@ -161,7 +179,7 @@
             current = sums[stage]
         else:
             mine[...] = total
-    me = exchange("depth", depth_size, mine, gathered, send_sems, recv_sems, offset, whole=True)
+    me = exchange([("depth", depth_size)], mine, gathered, send_sems, recv_sems, offset, whole=True)
     offset += depth_size
     gathered[me] = mine[...]
     summed = gathered[...].reshape(sketch_ref.shape)
@@ -171,9 +189,10 @@
         sketch, sketch, (((1,), (1,)), ((), ())), precision=lax.Precision.HIGHEST,
         preferred_element_type=jnp.float32,
     ) / row_total
-    for stage, (axis, size) in enumerate(stages):
+    for stage, group in enumerate(gram_groups):
         slot = gram_slots[stage]
-        me = exchange(axis, size, carried, slot, send_sems, recv_sems, offset, whole=True)
+        size = member_of(group)[1]
+        me = exchange(group, carried, slot, send_sems, recv_sems, offset, whole=True)
         offset += size
         slot[me] = carried[...]
         total = slot[0]
@@ -189,8 +208,10 @@
     rows, width = probe_all.shape
     scratch = [pltpu.VMEM(part.shape[stage:], jnp.float32) for stage in range(len(stages))]
     scratch += [pltpu.VMEM(part.shape[stage + 1 :], jnp.float32) for stage in range(len(stages) - 1)]
-    scratch += [pltpu.VMEM((size, rows, rows), jnp.float32) for _, size in stages]
-    semaphores = 2 * sum(size for _, size in stages) + depth_size
+    gram_groups = [stages[:2]] + [[stage] for stage in stages[2:]]
+    group_sizes = [math.prod(size for _, size in group) for group in gram_groups]
+    scratch += [pltpu.VMEM((size, rows, rows), jnp.float32) for size in group_sizes]
+    semaphores = sum(size for _, size in stages) + depth_size + sum(group_sizes)
     scratch += [
         pltpu.VMEM(part.shape[-2:], jnp.float32),
         pltpu.VMEM((depth_size,) + part.shape[-2:], jnp.float32),
@@ -199,7 +220,7 @@
         pltpu.SemaphoreType.DMA((semaphores,)),
     ]
     return pl.pallas_call(
-        lambda *refs: reduce_kernel(stages, depth_size, divisor, row_total, *refs),
+        lambda *refs: reduce_kernel(stages, gram_groups, depth_size, divisor, row_total, *refs),
         out_shape=(
             jax.ShapeDtypeStruct((rows, width), jnp.float32),
             jax.ShapeDtypeStruct((rows, rows), jnp.float32),

time: 147 us -> 148 us (level)
  the two profiles are of different devices: /device:TPU:1 before, /device:TPU:16 now
where the time goes in v3:
time: 148 us; the launch traced here: 147 us
  Pallas kernels  57.7 us (39%)
  other arithmetic  33.6 us (23%)
  local copies, waits for them, and re-layouts  28.4 us (19%)
  matrix products  13.7 us (9%)
  waiting for transfers between devices  4.9 us (3%)
  starting transfers between devices  4.29 us (3%)
  between operations  4.07 us (3%)
    pallas_call x1, Pallas kernels, reduce_all(): pl.pallas_call(lambda *refs: reduce_kernel(stages, gram_groups, depth_siz...  57.7 us
    reshape x2, local copies, waits for them, and re-layouts, shards(): by_axes = sketch_part.reshape(rows, planes, CHIPS_Y, CHIPS_Z, CORES, -1)  10.6 us
    another operation x3, other arithmetic, shards(): lower_factor = jnp.linalg.cholesky(gram_matrix)  6.52 us
    dot_general x20, matrix products, transform(): jnp.einsum('nscb,sbtd->ntdc', turned, matrix, preferred_element_type=jnp....  6.28 us
    dot_general x20, matrix products, transform(): jnp.einsum('nrab,rasc->nscb', grid_values, matrix, preferred_element_type...  5.76 us
    all_to_all x1, waiting for transfers between devices, shards(): payload = lax.all_to_all(payload, 'depth', 0, 0, tiled=True)  4.9 us
    another operation x1, other arithmetic, shards(): lax.linalg.triangular_solve(lower_factor, flattened, left_side=True, lowe...  4.89 us
    reshape x1, local copies, waits for them, and re-layouts, shards(): jnp.transpose(by_axes, (4, 3, 2, 0, 1, 5))  4.53 us
  transfers between devices with their start and end apart: 1, of which 1 were waited for; matrix products, arithmetic and copies ran while one was open for 2% of the time, Pallas kernels for 0%

profile of v3, /device:TPU:16, one launch (start us, length us, event | category | flops | bytes accessed | tf_op | source)
XLA Modules:
  0.0 146.8 jit_solution(18068021751052426795)
XLA Ops:
  0.6 1.4 reshape.1906
  2.1 0.8 constant_dynamic-slice_fusion
  3.0 0.9 convert_reduce_fusion.2
  4.3 0.5 broadcast.1731
  4.8 1.5 %reduce.15 = bf16[4,79872]{1,0:T(4,128)(2,1)S(1)} reduce(bf16[4,1,79872]{2,0,1:T(4,128)(2,1)S(1)} %maximum_bitcast_fusion, bf16[]{:T(256)} %broadcast.1731), dimensions={1}, to_apply=%copy.229.reduce_sub_computation | reduce | bytes 1277954 | tf_op jit(solution)/shard_map/all_to_all | solution.py:258
  6.3 1.3 reshape.2035
  7.6 4.3 %all-to-all-start = ((bf16[4,2,39936]{2,1,0:T(2,128)(2,1)}), bf16[4,2,39936]{2,1,0:T(2,128)(2,1)S(1)}, u32[]{:S(2)}, u32[]{:S(2)}) async-start(bf16[4,2,39936]{2,1,0:T(2,128)(2,1)} %reshape.2035), calls=%async_computation | async-start | bytes 1277952 | tf_op jit(solution)/shard_map/all_to_all | solution.py:258
  13.0 0.6 fusion.192
  17.7 4.9 %all-to-all-done = bf16[4,2,39936]{2,1,0:T(2,128)(2,1)S(1)} async-done(((bf16[4,2,39936]{2,1,0:T(2,128)(2,1)}), bf16[4,2,39936]{2,1,0:T(2,128)(2,1)S(1)}, u32[]{:S(2)}, u32[]{:S(2)}) %all-to-all-start) | async-done | bytes 639008 | tf_op jit(solution)/shard_map/all_to_all | solution.py:258
  22.6 0.7 reshape.2036
  23.3 0.5 copy.481
  24.2 0.7 copy.278.refs_1_
  24.9 1.0 fusion.223
  26.1 0.4 cos.176
  26.6 0.7 slice_bitcast_fusion.11
  27.4 0.6 convert_bitcast_fusion.4
  29.2 0.7 convert_bitcast_fusion.2
  31.1 0.7 convert_bitcast_fusion
  33.0 0.7 add_bitcast_fusion.2
  33.7 0.6 slice_bitcast_fusion.17
  34.3 0.6 slice_bitcast_fusion.18
  34.9 0.6 slice_bitcast_fusion.19
  35.6 0.6 copy.480
  36.2 0.8 reshape.1930
  37.0 1.4 fusion.38
  38.5 1.9 %multiply_bitcast_fusion.1 = (f32[1,16,1,64,64]{4,3,1,2,0:T(8,128)S(1)}, f32[1,16,1,64,64]{4,3,1,2,0:T(8,128)S(1)}, f32[16,1,64,64]{3,2,0,1:T(8,128)S(1)}, f32[1...) fusion(f32[16,4,64,64]{3,2,0,1:T(8,128)S(1)} %reshape.1930, ...), kind=kLoop, calls=%fused_computation.174 | loop fusion | flops 1048576 | bytes 2867204 | tf_op jit(solution)/shard_map/stack | solution.py:288
  42.0 0.4 convolution_bitcast_fusion.20
  46.5 0.4 convolution_bitcast_fusion.12
  47.3 0.5 copy-done.4
  47.8 0.7 bitcast_multiply_fusion
  49.2 0.6 convolution_bitcast_fusion.10
  51.0 0.7 fusion.11
  52.4 0.4 convolution_bitcast_fusion.6
  53.9 0.7 fusion.14
  56.4 0.4 convolution_bitcast_fusion
  56.8 0.7 bitcast_multiply_fusion.1
  57.8 3.7 %reshape.1925 = f32[16,4,8,8,2,32]{5,4,3,2,1,0:T(2,128)} reshape(f32[16,4,64,64]{3,2,1,0:T(8,128)S(1)} %pad_maximum_fusion) | data formatting | bytes 2097152 | tf_op jit(solution)/shard_map/reshape | solution.py:310
  61.6 6.9 %copy.479 = f32[16,4,8,8,2,32]{5,1,0,2,3,4:T(4,128)} copy(f32[16,4,8,8,2,32]{5,4,3,2,1,0:T(2,128)} %reshape.1925) | data formatting | bytes 2097152 | tf_op jit(solution)/shard_map/reshape | solution.py:310
  68.4 4.5 %reshape.1926.refs_0_ = f32[2,8,8,16,128]{4,3,2,1,0:T(8,128)} reshape(f32[2,8,8,16,4,32]{5,4,3,2,1,0:T(4,128)} %bitcast.694) | data formatting | bytes 2097152 | tf_op jit(solution)/shard_map/reshape | solution.py:312
  73.0 57.7 %shard_map.77 = (f32[64,128]{1,0:T(8,128)}, f32[64,64]{1,0:T(8,128)}) custom-call(f32[2,8,8,16,128]{4,3,2,1,0:T(8,128)} %reshape.1926.refs_0_, f32[64,128]{1,0:T(8,128)} %copy.278.refs_1_), custom_call_target="tpu_custom_call" | custom-call | tf_op jit(solution)/shard_map/pallas_call | solution.py:222
  130.7 0.8 copy.279
  131.5 0.8 fusion.148
  132.3 5.8 %cholesky.15 = f32[64,64]{1,0:T(8,128)S(1)} custom-call(f32[64,64]{1,0:T(8,128)S(1)} %fusion.148), custom_call_target="Cholesky" | custom-call | tf_op jit(solution)/shard_map/jit(cholesky)/cholesky | solution.py:323
  138.2 0.6 compare_reduce_fusion
  138.8 0.7 fusion.161
  139.5 0.7 copy.280
  140.2 4.9 %custom-call.6 = f32[1,64,64]{1,2,0:T(8,128)S(1)} custom-call(f32[1,64,64]{2,1,0:T(8,128)S(1)} %get-tuple-element.145), custom_call_target="InvertDiagBlocksLowerTriangular" | custom-call | tf_op jit(solution)/shard_map/triangular_solve | solution.py:324
  145.1 1.7 %convolution_bitcast_fusion.40 = f32[64,1,32]{0,2,1:T(8,128)} fusion(f32[1,64,64]{1,2,0:T(8,128)S(1)} %custom-call.6, f32[64,128]{1,0:T(8,128)} %get-tuple-element.5, s32[]{:T(128)S(6)} %select_n.358), kind=kOutput, calls=%fused_computation.42 | convolution fusion | flops 1572864 | bytes 57348 | tf_op jit(solution)/shard_map/triangular_solve | solution.py:324
  (145 shorter events, 18.6 us)
Async XLA Ops:
  4.3 8.7 %copy-start.20 = (f32[8]{0:T(128)S(1)}, f32[8]{0:T(128)}, u32[]{:S(2)}) copy-start(f32[8]{0:T(128)} %param.9) | copy-start | bytes 100
  4.3 11.7 %copy-start.13 = (f32[1,4,2,4096]{3,2,1,0:T(2,128)S(1)}, f32[1,4,2,4096]{3,2,1,0:T(2,128)}, u32[]{:S(2)}) copy-start(f32[1,4,2,4096]{3,2,1,0:T(2,128)} %param.6) | copy-start | bytes 393220
  7.6 15.0 %all-to-all-start = ((bf16[4,2,39936]{2,1,0:T(2,128)(2,1)}), bf16[4,2,39936]{2,1,0:T(2,128)(2,1)S(1)}, u32[]{:S(2)}, u32[]{:S(2)}) async-start(bf16[4,2,39936]{2,1,0:T(2,128)(2,1)} %reshape.2035), calls=%async_computation | async-start | bytes 1277952 | tf_op jit(solution)/shard_map/all_to_all | solution.py:258
  41.5 1.0 copy-start.11
  41.5 1.0 copy-start.12
  43.7 0.9 copy-start.9
  43.7 0.9 copy-start.10
  45.9 1.0 copy-start.7
  45.9 1.0 copy-start.8
  47.1 0.8 copy-start.4
  47.1 0.8 copy-start.5
  47.1 1.5 copy-start.18
  47.1 1.5 copy-start.19
  50.0 1.0 copy-start.2
  50.0 1.0 copy-start.3
  50.4 1.3 copy-start.16
  50.4 1.3 copy-start.17
  52.9 1.0 copy-start
  53.0 1.0 copy-start.1
  53.3 1.3 copy-start.14
  53.3 1.3 copy-start.15
  55.9 0.9 copy-start.6

commit v4 on v2

--- a/solution.py
+++ b/solution.py
@@ -255,11 +255,7 @@
     plane_screens = plane_screens.reshape(plane_screens.shape[:-1] + (SIDE, SIDE))
     born_scale = wave_nums * STEP_DEPTH
 
-    fields = []
-    current = sources
-    for plane in range(plane_count):
-        current = complex_times(plane_screens[:, plane], propagate(current, spectra, forward, inverse))
-        fields.append(current)
+    fields = [complex_times(plane_screens[:, 0], propagate(sources, spectra, forward, inverse))]
 
     def born(plane):
         scaled = born_scale[:, None, None, None] * probe_mine[None, :, plane]
@@ -268,10 +264,12 @@
 
     tangent = born(0)
     for plane in range(1, plane_count):
+        both = jnp.concatenate([fields[-1][:, None], tangent], axis=1)
         moved_on = complex_times(
-            plane_screens[:, plane][:, None], propagate(tangent, spectra[:, None], forward, inverse)
+            plane_screens[:, plane][:, None], propagate(both, spectra[:, None], forward, inverse)
         )
-        tangent = moved_on + born(plane)
+        fields.append(moved_on[:, 0])
+        tangent = moved_on[:, 1:] + born(plane)
 
     adjoint = tangent
     pieces = [None] * plane_count

time: 147 us -> 143 us (0.973)
  other arithmetic: 33.6 us -> 29.9 us
  local copies, waits for them, and re-layouts: 28.4 us -> 30.5 us
    another operation x18 -> x10, other arithmetic: 4.49 us -> 1.63 us  [complex_times(): return jnp.stack([real_part, imag_part], axis=-3)]
    another operation x17 -> x19, other arithmetic: 5.63 us -> 3.96 us
    mul x1 -> x3, other arithmetic: 0.66 us -> 2.17 us  [born(): -scaled * background[:, None, 1]]
    dot_general x20 -> x14, matrix products: 5.76 us -> 4.73 us  [transform(): jnp.einsum('nrab,rasc->nscb', grid_values, matrix, preferred_element_type...]
    unnamed x48 -> x38, local copies, waits for them, and re-layouts: 4.43 us -> 5.27 us
    dot_general x20 -> x14, matrix products: 6.28 us -> 5.98 us  [transform(): jnp.einsum('nscb,sbtd->ntdc', turned, matrix, preferred_element_type=jnp....]
  transfers between devices with their start and end apart: 1 -> 1, of which waited for: 1 -> 1; matrix products, arithmetic and copies ran while one was open for 2% -> 3% of each run, Pallas kernels for 0% -> 0%
where the time goes in v4:
time: 143 us; the launch traced here: 142 us
  Pallas kernels  59.6 us (42%)
  local copies, waits for them, and re-layouts  30.5 us (21%)
  other arithmetic  29.9 us (21%)
  matrix products  12.4 us (9%)
  starting transfers between devices  4.84 us (3%)
  between operations  3.93 us (3%)
    pallas_call x1, Pallas kernels, reduce_all(): pl.pallas_call(lambda *refs: reduce_kernel(stages, depth_size, divisor, r...  59.6 us
    reshape x2, local copies, waits for them, and re-layouts, shards(): by_axes = sketch_part.reshape(rows, planes, CHIPS_Y, CHIPS_Z, CORES, -1)  10.6 us
    another operation x3, other arithmetic, shards(): lower_factor = jnp.linalg.cholesky(gram_matrix)  6.52 us
    dot_general x14, matrix products, transform(): jnp.einsum('nscb,sbtd->ntdc', turned, matrix, preferred_element_type=jnp....  5.98 us
    unnamed x38, local copies, waits for them, and re-layouts  5.27 us
    another operation x1, other arithmetic, shards(): lax.linalg.triangular_solve(lower_factor, flattened, left_side=True, lowe...  4.89 us
    all_to_all x1, starting transfers between devices, shards(): payload = lax.all_to_all(payload, 'depth', 0, 0, tiled=True)  4.84 us
    dot_general x14, matrix products, transform(): jnp.einsum('nrab,rasc->nscb', grid_values, matrix, preferred_element_type...  4.73 us
  transfers between devices with their start and end apart: 1, of which 1 were waited for; matrix products, arithmetic and copies ran while one was open for 3% of the time, Pallas kernels for 0%

profile of v4, /device:TPU:1, one launch (start us, length us, event | category | flops | bytes accessed | tf_op | source)
XLA Modules:
  0.0 141.6 jit_solution(9639042947094653863)
XLA Ops:
  0.6 1.4 %reshape.1390 = bf16[4,65536]{1,0:T(4,128)(2,1)S(1)} reshape(bf16[64,1,4096]{2,0,1:T(8,128)(2,1)} %param.11) | data formatting | bytes 1048576 | tf_op jit(solution)/shard_map/reshape | solution.py:234
  2.1 0.8 constant_dynamic-slice_fusion
  3.5 0.5 broadcast.1414
  4.0 1.5 %reduce.15 = bf16[4,79872]{1,0:T(4,128)(2,1)S(1)} reduce(bf16[4,1,79872]{2,0,1:T(4,128)(2,1)S(1)} %maximum_bitcast_fusion, bf16[]{:T(256)} %broadcast.1414), dimensions={1}, to_apply=%copy.189.reduce_sub_computation | reduce | bytes 1277954 | tf_op jit(solution)/shard_map/all_to_all | solution.py:237
  5.5 1.3 reshape.1495
  6.8 4.8 %all-to-all-start = ((bf16[4,2,39936]{2,1,0:T(2,128)(2,1)}), bf16[4,2,39936]{2,1,0:T(2,128)(2,1)S(1)}, u32[]{:S(2)}, u32[]{:S(2)}) async-start(bf16[4,2,39936]{2,1,0:T(2,128)(2,1)} %reshape.1495), calls=%async_computation | async-start | bytes 1277952 | tf_op jit(solution)/shard_map/all_to_all | solution.py:237
  12.7 0.6 fusion.161
  17.3 0.8 convolution_bitcast_fusion.24
  18.1 0.6 slice_bitcast_fusion.9
  18.7 0.5 all-to-all-done
  19.2 0.7 reshape.1496
  19.9 0.5 copy.427
  20.7 0.7 copy.230.refs_1_
  21.5 1.0 fusion.182
  23.2 0.7 slice_bitcast_fusion.13
  23.9 0.7 slice_bitcast_fusion.4
  24.6 0.6 slice_bitcast_fusion.25
  25.2 0.6 slice_bitcast_fusion.24
  25.9 0.6 slice_bitcast_fusion.23
  26.5 0.6 copy.426
  27.1 0.8 reshape.1414
  28.0 0.8 fusion.181
  28.8 0.7 multiply_convert_fusion.1
  30.2 0.4 convolution_bitcast_fusion.10
  31.3 0.4 convolution_bitcast_fusion.8
  32.3 0.7 negate_multiply_fusion.2
  33.8 0.4 convolution_bitcast_fusion.6
  34.9 0.4 convolution_bitcast_fusion.4
  35.9 0.7 negate_multiply_fusion.1
  38.5 0.4 convolution_bitcast_fusion
  39.5 0.7 negate_multiply_fusion
  40.5 0.7 fusion.39
  43.7 0.7 fusion.41
  44.7 0.5 convolution_bitcast_fusion.19
  46.9 0.7 fusion.43
  49.8 0.7 fusion.32
  50.8 3.8 %reshape.1409 = f32[16,4,8,8,2,32]{5,4,3,2,0,1:T(2,128)} reshape(f32[16,4,64,64]{3,2,0,1:T(8,128)S(1)} %pad_maximum_fusion) | data formatting | bytes 2097152 | tf_op jit(solution)/shard_map/reshape | solution.py:287
  54.5 6.8 %copy.425 = f32[16,4,8,8,2,32]{5,1,0,2,3,4:T(4,128)} copy(f32[16,4,8,8,2,32]{5,4,3,2,0,1:T(2,128)} %reshape.1409) | data formatting | bytes 2097152 | tf_op jit(solution)/shard_map/reshape | solution.py:287
  61.4 4.5 %reshape.1410.refs_0_ = f32[2,8,8,16,128]{4,3,2,1,0:T(8,128)} reshape(f32[2,8,8,16,4,32]{5,4,3,2,1,0:T(4,128)} %bitcast.538) | data formatting | bytes 2097152 | tf_op jit(solution)/shard_map/reshape | solution.py:289
  65.9 59.6 %shard_map.77 = (f32[64,128]{1,0:T(8,128)}, f32[64,64]{1,0:T(8,128)}) custom-call(f32[2,8,8,16,128]{4,3,2,1,0:T(8,128)} %reshape.1410.refs_0_, f32[64,128]{1,0:T(8,128)} %copy.230.refs_1_), custom_call_target="tpu_custom_call" | custom-call | tf_op jit(solution)/shard_map/pallas_call | solution.py:201
  125.5 0.8 copy.231
  126.3 0.8 fusion.135
  127.1 5.8 %cholesky.15 = f32[64,64]{1,0:T(8,128)S(1)} custom-call(f32[64,64]{1,0:T(8,128)S(1)} %fusion.135), custom_call_target="Cholesky" | custom-call | tf_op jit(solution)/shard_map/jit(cholesky)/cholesky | solution.py:300
  133.0 0.6 compare_reduce_fusion
  133.6 0.7 fusion.148
  134.3 0.7 copy.232
  135.0 4.9 %custom-call.6 = f32[1,64,64]{1,2,0:T(8,128)S(1)} custom-call(f32[1,64,64]{2,1,0:T(8,128)S(1)} %get-tuple-element.126), custom_call_target="InvertDiagBlocksLowerTriangular" | custom-call | tf_op jit(solution)/shard_map/triangular_solve | solution.py:301
  139.9 1.7 %convolution_bitcast_fusion.28 = f32[64,1,32]{0,2,1:T(8,128)} fusion(f32[1,64,64]{1,2,0:T(8,128)S(1)} %custom-call.6, f32[64,128]{1,0:T(8,128)} %get-tuple-element.5, s32[]{:T(128)S(6)} %select_n.286), kind=kOutput, calls=%fused_computation.32 | convolution fusion | flops 1572864 | bytes 57348 | tf_op jit(solution)/shard_map/triangular_solve | solution.py:301
  (125 shorter events, 17.2 us)
Async XLA Ops:
  0.6 2.4 %copy-start.14 = (f32[1,4096]{1,0:T(1,128)S(1)}, f32[1,4096]{1,0:T(1,128)}, u32[]{:S(2)}) copy-start(f32[1,4096]{1,0:T(1,128)} %param.10) | copy-start | bytes 49156
  5.5 7.2 %copy-start.15 = (f32[8]{0:T(128)S(1)}, f32[8]{0:T(128)}, u32[]{:S(2)}) copy-start(f32[8]{0:T(128)} %param.9) | copy-start | bytes 100
  5.5 10.2 %copy-start.7 = (f32[1,4,2,4096]{3,2,1,0:T(2,128)S(1)}, f32[1,4,2,4096]{3,2,1,0:T(2,128)}, u32[]{:S(2)}) copy-start(f32[1,4,2,4096]{3,2,1,0:T(2,128)} %param.6) | copy-start | bytes 393220
  6.8 12.4 %all-to-all-start = ((bf16[4,2,39936]{2,1,0:T(2,128)(2,1)}), bf16[4,2,39936]{2,1,0:T(2,128)(2,1)S(1)}, u32[]{:S(2)}, u32[]{:S(2)}) async-start(bf16[4,2,39936]{2,1,0:T(2,128)(2,1)} %reshape.1495), calls=%async_computation | async-start | bytes 1277952 | tf_op jit(solution)/shard_map/all_to_all | solution.py:237
  31.3 0.8 copy-start.5
  31.3 0.8 copy-start.6
  34.9 0.8 copy-start.3
  34.9 0.8 copy-start.4
  38.5 0.8 copy-start.1
  38.5 0.8 copy-start.2
  40.4 0.8 copy-start.12
  40.4 0.8 copy-start.13
  41.9 0.8 copy-start
  43.7 0.8 copy-start.10
  43.7 0.8 copy-start.11
  46.9 0.8 copy-start.8
  46.9 0.8 copy-start.9

commit v5 on v4

--- a/solution.py
+++ b/solution.py
@@ -229,20 +229,24 @@
     rest = slowness - high.astype(jnp.float32)
     middle = rest.astype(jnp.bfloat16)
     low = (rest - middle.astype(jnp.float32)).astype(jnp.bfloat16)
-    shared = jnp.concatenate([probe_slab.reshape(-1), high.reshape(-1), middle.reshape(-1), low.reshape(-1)])
+    slab_size = probe_count * slab_points
+    slab_rows = -(-slab_size // points)
+    slab_row = jnp.pad(probe_slab.reshape(-1), (0, slab_rows * points - slab_size)).reshape(slab_rows, points)
+    shared = jnp.concatenate([slab_row, high, middle, low], axis=0)
     payload = jnp.concatenate(
-        [probes.reshape(depth_count, -1), jnp.broadcast_to(shared[None], (depth_count,) + shared.shape)],
+        [
+            probes.reshape(depth_count, rows, points),
+            jnp.broadcast_to(shared[None], (depth_count,) + shared.shape),
+        ],
         axis=1,
     )
     payload = lax.all_to_all(payload, "depth", 0, 0, tiled=True)
-    cut = rows * points
-    probe_mine = jnp.transpose(payload[:, :cut].reshape(depth_count, rows, points), (1, 0, 2))
-    probe_mine = probe_mine.astype(jnp.float32)
+    probe_mine = jnp.transpose(payload[:, :rows], (1, 0, 2)).astype(jnp.float32)
     probe_mine = probe_mine.reshape(probe_mine.shape[:2] + (SIDE, SIDE))
-    slab_size = probe_count * slab_points
-    probe_all = payload[:, cut : cut + slab_size].reshape(depth_count, probe_count, slab_points)
+    probe_all = payload[:, rows : rows + slab_rows].reshape(depth_count, -1)[:, :slab_size]
+    probe_all = probe_all.reshape(depth_count, probe_count, slab_points)
     probe_all = jnp.transpose(probe_all, (1, 0, 2)).reshape(probe_count, -1).astype(jnp.float32)
-    parts = payload[:, cut + slab_size :].reshape(depth_count, 3, points).astype(jnp.float32)
+    parts = payload[:, rows + slab_rows :].astype(jnp.float32)
     slowness_all = (parts[:, 0] + parts[:, 1]) + parts[:, 2]
     plane_count = slowness_all.shape[0]
     sources = encoded_sources(incident, encode, incident.shape[1])

time: 143 us -> 143 us (level)
  local copies, waits for them, and re-layouts: 30.5 us -> 25 us
  other arithmetic: 29.9 us -> 33.9 us
    unnamed x38 -> x33, local copies, waits for them, and re-layouts: 5.27 us -> 2.11 us
    sin x1, other arithmetic: 1.05 us -> 3.23 us  [screens(): return jnp.stack([jnp.cos(phase), jnp.sin(phase)], axis=2)]
    concatenate x1 -> x2, other arithmetic: 0.01 us -> 2.12 us  [the longest x1 2.03 us: shards(): jnp.concatenate([probes.reshape(depth_count, rows, points), jnp.broadcast...]
    all_to_all x2 -> x0, other arithmetic: 1.84 us -> none  [shards(): payload = lax.all_to_all(payload, 'depth', 0, 0, tiled=True)]
where the time goes in v5:
time: 143 us; the launch traced here: 141 us
  Pallas kernels  60.1 us (42%)
  other arithmetic  33.9 us (24%)
  local copies, waits for them, and re-layouts  25 us (17%)
  matrix products  12.1 us (8%)
  starting transfers between devices  4.97 us (3%)
  between operations  4.1 us (3%)
    pallas_call x1, Pallas kernels, reduce_all(): pl.pallas_call(lambda *refs: reduce_kernel(stages, depth_size, divisor, r...  60.1 us
    reshape x2, local copies, waits for them, and re-layouts, shards(): by_axes = sketch_part.reshape(rows, planes, CHIPS_Y, CHIPS_Z, CORES, -1)  10.6 us
    another operation x3, other arithmetic, shards(): lower_factor = jnp.linalg.cholesky(gram_matrix)  6.52 us
    dot_general x14, matrix products, transform(): jnp.einsum('nscb,sbtd->ntdc', turned, matrix, preferred_element_type=jnp....  5.97 us
    all_to_all x1, starting transfers between devices, shards(): payload = lax.all_to_all(payload, 'depth', 0, 0, tiled=True)  4.97 us
    another operation x1, other arithmetic, shards(): lax.linalg.triangular_solve(lower_factor, flattened, left_side=True, lowe...  4.89 us
    reshape x1, local copies, waits for them, and re-layouts, shards(): jnp.transpose(by_axes, (4, 3, 2, 0, 1, 5))  4.53 us
    dot_general x14, matrix products, transform(): jnp.einsum('nrab,rasc->nscb', grid_values, matrix, preferred_element_type...  4.5 us
  transfers between devices with their start and end apart: 1, of which 1 were waited for; matrix products, arithmetic and copies ran while one was open for 3% of the time, Pallas kernels for 0%

profile of v5, /device:TPU:1, one launch (start us, length us, event | category | flops | bytes accessed | tf_op | source)
XLA Modules:
  0.0 141.3 jit_solution(11088557258567191581)
XLA Ops:
  0.6 0.8 constant_dynamic-slice_fusion
  1.6 0.8 fusion.186
  2.5 2.0 %pad_maximum_fusion.3 = bf16[4,20,4096]{2,1,0:T(8,128)(2,1)} fusion(bf16[4,4,4096]{2,1,0:T(4,128)(2,1)S(1)} %broadcast_in_dim.11, bf16[4,16,4096]{2,1,0:T(8,128)(2,1)} %bitcast.525), kind=kLoop, calls=%fused_computation.42 | loop fusion | flops 1310720 | bytes 1310720 | tf_op jit(solution)/shard_map/concatenate | solution.py:236
  4.6 5.0 %all-to-all-start = ((bf16[4,20,4096]{2,1,0:T(8,128)(2,1)}), bf16[4,20,4096]{2,1,0:T(8,128)(2,1)S(1)}, u32[]{:S(2)}, u32[]{:S(2)}) async-start(bf16[4,20,4096]{2,1,0:T(8,128)(2,1)} %pad_maximum_fusion.3), calls=%async_computation | async-start | bytes 1572864 | tf_op jit(solution)/shard_map/all_to_all | solution.py:243
  10.7 0.7 fusion.161
  15.4 0.8 convolution_bitcast_fusion.24
  16.2 0.6 slice_bitcast_fusion.9
  16.8 1.1 all-to-all-done
  18.2 0.7 copy.187.refs_1_
  18.9 3.2 %sine_reduce_fusion = (f32[4,4096]{1,0:T(4,128)S(1)}, f32[4,4096]{1,0:T(4,128)S(1)}) fusion(f32[4,3,4096]{2,1,0:T(4,128)S(1)} %slice_convert_fusion, f32[]{:T(128)} %fusion.161), kind=kLoop, calls=%fused_computation.253 | loop fusion | flops 49152 | bytes 327684 | tf_op jit(solution)/shard_map/sin | solution.py:87
  22.4 0.7 slice_bitcast_fusion.13
  23.1 0.6 slice_bitcast_fusion.4
  23.8 0.6 slice_bitcast_fusion.25
  24.4 0.6 slice_bitcast_fusion.24
  25.1 0.6 slice_bitcast_fusion.23
  25.8 0.8 reshape.1401
  26.6 0.8 fusion.182
  27.4 0.8 multiply_convert_fusion.1
  28.9 0.4 convolution_bitcast_fusion.10
  30.0 0.4 convolution_bitcast_fusion.8
  31.0 0.8 negate_multiply_fusion.2
  32.6 0.4 convolution_bitcast_fusion.6
  33.7 0.4 convolution_bitcast_fusion.4
  34.6 0.8 negate_multiply_fusion.1
  36.2 0.4 convolution_bitcast_fusion.2
  37.4 0.4 convolution_bitcast_fusion
  38.3 0.8 negate_multiply_fusion
  39.4 0.8 fusion.39
  40.9 0.4 convolution_bitcast_fusion.22
  42.3 0.4 convolution_bitcast_fusion.20
  42.7 0.8 fusion.41
  44.2 0.4 convolution_bitcast_fusion.18
  45.7 0.8 fusion.43
  47.2 0.4 convolution_bitcast_fusion.14
  48.5 0.4 convolution_bitcast_fusion.12
  48.9 0.8 fusion.32
  50.0 3.7 %reshape.1396 = f32[16,4,8,8,2,32]{5,4,3,2,0,1:T(2,128)} reshape(f32[16,4,64,64]{3,2,0,1:T(8,128)S(1)} %pad_maximum_fusion) | data formatting | bytes 2097152 | tf_op jit(solution)/shard_map/reshape | solution.py:291
  53.7 6.9 %copy.380 = f32[16,4,8,8,2,32]{5,1,0,2,3,4:T(4,128)} copy(f32[16,4,8,8,2,32]{5,4,3,2,0,1:T(2,128)} %reshape.1396) | data formatting | bytes 2097152 | tf_op jit(solution)/shard_map/reshape | solution.py:291
  60.6 4.5 %reshape.1397.refs_0_ = f32[2,8,8,16,128]{4,3,2,1,0:T(8,128)} reshape(f32[2,8,8,16,4,32]{5,4,3,2,1,0:T(4,128)} %bitcast.524) | data formatting | bytes 2097152 | tf_op jit(solution)/shard_map/reshape | solution.py:293
  65.1 60.1 %shard_map.77 = (f32[64,128]{1,0:T(8,128)}, f32[64,64]{1,0:T(8,128)}) custom-call(f32[2,8,8,16,128]{4,3,2,1,0:T(8,128)} %reshape.1397.refs_0_, f32[64,128]{1,0:T(8,128)} %copy.187.refs_1_), custom_call_target="tpu_custom_call" | custom-call | tf_op jit(solution)/shard_map/pallas_call | solution.py:201
  125.2 0.8 copy.188
  126.1 0.8 fusion.135
  126.8 5.8 %cholesky.15 = f32[64,64]{1,0:T(8,128)S(1)} custom-call(f32[64,64]{1,0:T(8,128)S(1)} %fusion.135), custom_call_target="Cholesky" | custom-call | tf_op jit(solution)/shard_map/jit(cholesky)/cholesky | solution.py:304
  132.7 0.6 compare_reduce_fusion
  133.4 0.7 fusion.148
  134.0 0.7 copy.189
  134.7 4.9 %custom-call.6 = f32[1,64,64]{1,2,0:T(8,128)S(1)} custom-call(f32[1,64,64]{2,1,0:T(8,128)S(1)} %get-tuple-element.121), custom_call_target="InvertDiagBlocksLowerTriangular" | custom-call | tf_op jit(solution)/shard_map/triangular_solve | solution.py:305
  139.6 1.7 %convolution_bitcast_fusion.28 = f32[64,1,32]{0,2,1:T(8,128)} fusion(f32[1,64,64]{1,2,0:T(8,128)S(1)} %custom-call.6, f32[64,128]{1,0:T(8,128)} %get-tuple-element.5, s32[]{:T(128)S(6)} %select_n.286), kind=kOutput, calls=%fused_computation.32 | convolution fusion | flops 1572864 | bytes 57348 | tf_op jit(solution)/shard_map/triangular_solve | solution.py:305
  (119 shorter events, 14.4 us)
Async XLA Ops:
  4.6 6.1 %copy-start.14 = (f32[8]{0:T(128)S(1)}, f32[8]{0:T(128)}, u32[]{:S(2)}) copy-start(f32[8]{0:T(128)} %param.9) | copy-start | bytes 100
  4.6 9.3 %copy-start.7 = (f32[1,4,2,4096]{3,2,1,0:T(2,128)S(1)}, f32[1,4,2,4096]{3,2,1,0:T(2,128)}, u32[]{:S(2)}) copy-start(f32[1,4,2,4096]{3,2,1,0:T(2,128)} %param.6) | copy-start | bytes 393220
  4.6 13.3 %all-to-all-start = ((bf16[4,20,4096]{2,1,0:T(8,128)(2,1)}), bf16[4,20,4096]{2,1,0:T(8,128)(2,1)S(1)}, u32[]{:S(2)}, u32[]{:S(2)}) async-start(bf16[4,20,4096]{2,1,0:T(8,128)(2,1)} %pad_maximum_fusion.3), calls=%async_computation | async-start | bytes 1572864 | tf_op jit(solution)/shard_map/all_to_all | solution.py:243
  30.0 0.8 copy-start.5
  30.0 0.8 copy-start.6
  33.7 0.8 copy-start.3
  33.7 0.8 copy-start.4
  37.3 0.8 copy-start.1
  37.3 0.8 copy-start.2
  39.4 0.8 copy-start.12
  39.4 0.8 copy-start.13
  40.9 0.8 copy-start
  42.7 0.8 copy-start.10
  42.7 0.8 copy-start.11
  45.7 0.8 copy-start.8
  45.7 0.8 copy-start.9

commit v6 on v4

--- a/solution.py
+++ b/solution.py
@@ -101,34 +101,36 @@
     return jnp.sum(onehot_rows * wavenum[None, :], axis=1)
 
 
-def exchange(axis, size, current, slot, send_sems, recv_sems, offset, whole=False):
+def exchange(axis, size, current, slot, send_sems, recv_sems, offset, whole=False, pieces=1):
     me = lax.axis_index(axis)
+
+    def copy_of(peer, piece, slot_index, source):
+        block = current if whole else current.at[source]
+        target = slot.at[slot_index]
+        if pieces > 1:
+            block, target = block.at[piece], target.at[piece]
+        return pltpu.make_async_remote_copy(
+            src_ref=block,
+            dst_ref=target,
+            send_sem=send_sems.at[offset + source * pieces + piece],
+            recv_sem=recv_sems.at[offset + slot_index * pieces + piece],
+            device_id={axis: peer},
+            device_id_type=pl.DeviceIdType.MESH,
+        )
+
     copies = []
     for step in range(1, size):
         peer = lax.rem(me + step, size)
-        copy = pltpu.make_async_remote_copy(
-            src_ref=current if whole else current.at[peer],
-            dst_ref=slot.at[me],
-            send_sem=send_sems.at[offset + peer],
-            recv_sem=recv_sems.at[offset + me],
-            device_id={axis: peer},
-            device_id_type=pl.DeviceIdType.MESH,
-        )
-        copy.start()
-        copies.append(copy)
+        for piece in range(pieces):
+            copy = copy_of(peer, piece, me, peer)
+            copy.start()
+            copies.append(copy)
     for copy in copies:
         copy.wait_send()
     for step in range(1, size):
         sender = lax.rem(me + size - step, size)
-        incoming = pltpu.make_async_remote_copy(
-            src_ref=current if whole else current.at[sender],
-            dst_ref=slot.at[sender],
-            send_sem=send_sems.at[offset + sender],
-            recv_sem=recv_sems.at[offset + sender],
-            device_id={axis: sender},
-            device_id_type=pl.DeviceIdType.MESH,
-        )
-        incoming.wait_recv()
+        for piece in range(pieces):
+            copy_of(sender, piece, sender, sender).wait_recv()
     return me
 
 
@@ -151,8 +153,9 @@
     current = part_ref
     offset = 0
     for stage, (axis, size) in enumerate(stages):
-        me = exchange(axis, size, current, slots[stage], send_sems, recv_sems, offset)
-        offset += size
+        pieces = current.shape[1] if stage == 0 else 1
+        me = exchange(axis, size, current, slots[stage], send_sems, recv_sems, offset, pieces=pieces)
+        offset += size * pieces
         total = current[me]
         for step in range(1, size):
             total = total + slots[stage][lax.rem(me + size - step, size)]
@@ -190,7 +193,7 @@
     scratch = [pltpu.VMEM(part.shape[stage:], jnp.float32) for stage in range(len(stages))]
     scratch += [pltpu.VMEM(part.shape[stage + 1 :], jnp.float32) for stage in range(len(stages) - 1)]
     scratch += [pltpu.VMEM((size, rows, rows), jnp.float32) for _, size in stages]
-    semaphores = 2 * sum(size for _, size in stages) + depth_size
+    semaphores = 2 * sum(size for _, size in stages) + depth_size + stages[0][1] * part.shape[1]
     scratch += [
         pltpu.VMEM(part.shape[-2:], jnp.float32),
         pltpu.VMEM((depth_size,) + part.shape[-2:], jnp.float32),

time: 143 us -> 143 us (level)
  no operation moved by 1% of the time
where the time goes in v6:
time: 143 us; the launch traced here: 141 us
  Pallas kernels  59.5 us (42%)
  local copies, waits for them, and re-layouts  30.5 us (21%)
  other arithmetic  29.9 us (21%)
  matrix products  12.4 us (9%)
  starting transfers between devices  4.84 us (3%)
  between operations  3.93 us (3%)
    pallas_call x1, Pallas kernels, reduce_all(): pl.pallas_call(lambda *refs: reduce_kernel(stages, depth_size, divisor, r...  59.5 us
    reshape x2, local copies, waits for them, and re-layouts, shards(): by_axes = sketch_part.reshape(rows, planes, CHIPS_Y, CHIPS_Z, CORES, -1)  10.6 us
    another operation x3, other arithmetic, shards(): lower_factor = jnp.linalg.cholesky(gram_matrix)  6.52 us
    dot_general x14, matrix products, transform(): jnp.einsum('nscb,sbtd->ntdc', turned, matrix, preferred_element_type=jnp....  5.98 us
    unnamed x38, local copies, waits for them, and re-layouts  5.27 us
    another operation x1, other arithmetic, shards(): lax.linalg.triangular_solve(lower_factor, flattened, left_side=True, lowe...  4.89 us
    all_to_all x1, starting transfers between devices, shards(): payload = lax.all_to_all(payload, 'depth', 0, 0, tiled=True)  4.84 us
    dot_general x14, matrix products, transform(): jnp.einsum('nrab,rasc->nscb', grid_values, matrix, preferred_element_type...  4.73 us
  transfers between devices with their start and end apart: 1, of which 1 were waited for; matrix products, arithmetic and copies ran while one was open for 3% of the time, Pallas kernels for 0%

profile of v6, /device:TPU:1, one launch (start us, length us, event | category | flops | bytes accessed | tf_op | source)
XLA Modules:
  0.0 141.5 jit_solution(9439902289584538902)
XLA Ops:
  0.6 1.4 %reshape.1390 = bf16[4,65536]{1,0:T(4,128)(2,1)S(1)} reshape(bf16[64,1,4096]{2,0,1:T(8,128)(2,1)} %param.11) | data formatting | bytes 1048576 | tf_op jit(solution)/shard_map/reshape | solution.py:237
  2.1 0.8 constant_dynamic-slice_fusion
  3.5 0.5 broadcast.1414
  4.0 1.5 %reduce.15 = bf16[4,79872]{1,0:T(4,128)(2,1)S(1)} reduce(bf16[4,1,79872]{2,0,1:T(4,128)(2,1)S(1)} %maximum_bitcast_fusion, bf16[]{:T(256)} %broadcast.1414), dimensions={1}, to_apply=%copy.189.reduce_sub_computation | reduce | bytes 1277954 | tf_op jit(solution)/shard_map/all_to_all | solution.py:240
  5.5 1.3 reshape.1495
  6.8 4.8 %all-to-all-start = ((bf16[4,2,39936]{2,1,0:T(2,128)(2,1)}), bf16[4,2,39936]{2,1,0:T(2,128)(2,1)S(1)}, u32[]{:S(2)}, u32[]{:S(2)}) async-start(bf16[4,2,39936]{2,1,0:T(2,128)(2,1)} %reshape.1495), calls=%async_computation | async-start | bytes 1277952 | tf_op jit(solution)/shard_map/all_to_all | solution.py:240
  12.7 0.6 fusion.161
  17.3 0.8 convolution_bitcast_fusion.24
  18.1 0.6 slice_bitcast_fusion.9
  18.7 0.5 all-to-all-done
  19.2 0.7 reshape.1496
  19.9 0.5 copy.427
  20.7 0.7 copy.230.refs_1_
  21.5 1.0 fusion.182
  23.2 0.7 slice_bitcast_fusion.13
  23.9 0.7 slice_bitcast_fusion.4
  24.6 0.6 slice_bitcast_fusion.25
  25.2 0.6 slice_bitcast_fusion.24
  25.9 0.6 slice_bitcast_fusion.23
  26.5 0.6 copy.426
  27.1 0.8 reshape.1414
  28.0 0.8 fusion.181
  28.8 0.7 multiply_convert_fusion.1
  30.2 0.4 convolution_bitcast_fusion.10
  31.3 0.4 convolution_bitcast_fusion.8
  32.3 0.7 negate_multiply_fusion.2
  33.8 0.4 convolution_bitcast_fusion.6
  34.9 0.4 convolution_bitcast_fusion.4
  35.9 0.7 negate_multiply_fusion.1
  38.5 0.4 convolution_bitcast_fusion
  39.5 0.7 negate_multiply_fusion
  40.5 0.7 fusion.39
  43.7 0.7 fusion.41
  44.7 0.5 convolution_bitcast_fusion.19
  46.9 0.7 fusion.43
  49.8 0.7 fusion.32
  50.8 3.8 %reshape.1409 = f32[16,4,8,8,2,32]{5,4,3,2,0,1:T(2,128)} reshape(f32[16,4,64,64]{3,2,0,1:T(8,128)S(1)} %pad_maximum_fusion) | data formatting | bytes 2097152 | tf_op jit(solution)/shard_map/reshape | solution.py:290
  54.5 6.8 %copy.425 = f32[16,4,8,8,2,32]{5,1,0,2,3,4:T(4,128)} copy(f32[16,4,8,8,2,32]{5,4,3,2,0,1:T(2,128)} %reshape.1409) | data formatting | bytes 2097152 | tf_op jit(solution)/shard_map/reshape | solution.py:290
  61.4 4.5 %reshape.1410.refs_0_ = f32[2,8,8,16,128]{4,3,2,1,0:T(8,128)} reshape(f32[2,8,8,16,4,32]{5,4,3,2,1,0:T(4,128)} %bitcast.538) | data formatting | bytes 2097152 | tf_op jit(solution)/shard_map/reshape | solution.py:292
  65.9 59.5 %shard_map.77 = (f32[64,128]{1,0:T(8,128)}, f32[64,64]{1,0:T(8,128)}) custom-call(f32[2,8,8,16,128]{4,3,2,1,0:T(8,128)} %reshape.1410.refs_0_, f32[64,128]{1,0:T(8,128)} %copy.230.refs_1_), custom_call_target="tpu_custom_call" | custom-call | tf_op jit(solution)/shard_map/pallas_call | solution.py:204
  125.4 0.8 copy.231
  126.3 0.8 fusion.135
  127.0 5.8 %cholesky.15 = f32[64,64]{1,0:T(8,128)S(1)} custom-call(f32[64,64]{1,0:T(8,128)S(1)} %fusion.135), custom_call_target="Cholesky" | custom-call | tf_op jit(solution)/shard_map/jit(cholesky)/cholesky | solution.py:303
  132.9 0.6 compare_reduce_fusion
  133.6 0.7 fusion.148
  134.2 0.7 copy.232
  134.9 4.9 %custom-call.6 = f32[1,64,64]{1,2,0:T(8,128)S(1)} custom-call(f32[1,64,64]{2,1,0:T(8,128)S(1)} %get-tuple-element.126), custom_call_target="InvertDiagBlocksLowerTriangular" | custom-call | tf_op jit(solution)/shard_map/triangular_solve | solution.py:304
  139.8 1.7 %convolution_bitcast_fusion.28 = f32[64,1,32]{0,2,1:T(8,128)} fusion(f32[1,64,64]{1,2,0:T(8,128)S(1)} %custom-call.6, f32[64,128]{1,0:T(8,128)} %get-tuple-element.5, s32[]{:T(128)S(6)} %select_n.286), kind=kOutput, calls=%fused_computation.32 | convolution fusion | flops 1572864 | bytes 57348 | tf_op jit(solution)/shard_map/triangular_solve | solution.py:304
  (125 shorter events, 17.2 us)
Async XLA Ops:
  0.6 2.4 %copy-start.14 = (f32[1,4096]{1,0:T(1,128)S(1)}, f32[1,4096]{1,0:T(1,128)}, u32[]{:S(2)}) copy-start(f32[1,4096]{1,0:T(1,128)} %param.10) | copy-start | bytes 49156
  5.5 7.2 %copy-start.15 = (f32[8]{0:T(128)S(1)}, f32[8]{0:T(128)}, u32[]{:S(2)}) copy-start(f32[8]{0:T(128)} %param.9) | copy-start | bytes 100
  5.5 10.2 %copy-start.7 = (f32[1,4,2,4096]{3,2,1,0:T(2,128)S(1)}, f32[1,4,2,4096]{3,2,1,0:T(2,128)}, u32[]{:S(2)}) copy-start(f32[1,4,2,4096]{3,2,1,0:T(2,128)} %param.6) | copy-start | bytes 393220
  6.8 12.4 %all-to-all-start = ((bf16[4,2,39936]{2,1,0:T(2,128)(2,1)}), bf16[4,2,39936]{2,1,0:T(2,128)(2,1)S(1)}, u32[]{:S(2)}, u32[]{:S(2)}) async-start(bf16[4,2,39936]{2,1,0:T(2,128)(2,1)} %reshape.1495), calls=%async_computation | async-start | bytes 1277952 | tf_op jit(solution)/shard_map/all_to_all | solution.py:240
  31.3 0.8 copy-start.5
  31.3 0.8 copy-start.6
  34.9 0.8 copy-start.3
  34.9 0.8 copy-start.4
  38.5 0.8 copy-start.1
  38.5 0.8 copy-start.2
  40.4 0.8 copy-start.12
  40.4 0.8 copy-start.13
  41.9 0.8 copy-start
  43.7 0.8 copy-start.10
  43.7 0.8 copy-start.11
  46.9 0.8 copy-start.8
  46.9 0.8 copy-start.9

commit v7 on v4

--- a/solution.py
+++ b/solution.py
@@ -297,7 +297,7 @@
     depth_index = lax.axis_index("depth")
     flattened = lax.dynamic_slice_in_dim(sketch_all, depth_index * slab_width, slab_width, 1)
     local_planes = 1
-    lower_factor = jnp.linalg.cholesky(gram_matrix)
+    lower_factor = lax.linalg.cholesky(gram_matrix, symmetrize_input=False)
     sketch_basis = lax.linalg.triangular_solve(
         lower_factor, flattened, left_side=True, lower=True
     ).reshape(probe_count, local_planes, slab_width)

time: 143 us -> 142 us (level)
  no operation moved by 1% of the time
where the time goes in v7:
time: 142 us; the launch traced here: 141 us
  Pallas kernels  59.6 us (42%)
  other arithmetic  29.8 us (21%)
  local copies, waits for them, and re-layouts  29.6 us (21%)
  matrix products  12.4 us (9%)
  starting transfers between devices  4.84 us (3%)
  between operations  3.93 us (3%)
    pallas_call x1, Pallas kernels, reduce_all(): pl.pallas_call(lambda *refs: reduce_kernel(stages, depth_size, divisor, r...  59.6 us
    reshape x2, local copies, waits for them, and re-layouts, shards(): by_axes = sketch_part.reshape(rows, planes, CHIPS_Y, CHIPS_Z, CORES, -1)  10.6 us
    another operation x3, other arithmetic, shards(): lower_factor = lax.linalg.cholesky(gram_matrix, symmetrize_input=False)  7.27 us
    dot_general x14, matrix products, transform(): jnp.einsum('nscb,sbtd->ntdc', turned, matrix, preferred_element_type=jnp....  5.98 us
    unnamed x38, local copies, waits for them, and re-layouts  5.27 us
    another operation x1, other arithmetic, shards(): lax.linalg.triangular_solve(lower_factor, flattened, left_side=True, lowe...  4.89 us
    all_to_all x1, starting transfers between devices, shards(): payload = lax.all_to_all(payload, 'depth', 0, 0, tiled=True)  4.84 us
    dot_general x14, matrix products, transform(): jnp.einsum('nrab,rasc->nscb', grid_values, matrix, preferred_element_type...  4.73 us
  transfers between devices with their start and end apart: 1, of which 1 were waited for; matrix products, arithmetic and copies ran while one was open for 3% of the time, Pallas kernels for 0%

profile of v7, /device:TPU:1, one launch (start us, length us, event | category | flops | bytes accessed | tf_op | source)
XLA Modules:
  0.0 140.7 jit_solution(4757153971200697689)
XLA Ops:
  0.6 1.4 %reshape.1389 = bf16[4,65536]{1,0:T(4,128)(2,1)S(1)} reshape(bf16[64,1,4096]{2,0,1:T(8,128)(2,1)} %param.11) | data formatting | bytes 1048576 | tf_op jit(solution)/shard_map/reshape | solution.py:234
  2.1 0.8 constant_dynamic-slice_fusion
  3.5 0.5 broadcast.1402
  4.0 1.5 %reduce.13 = bf16[4,79872]{1,0:T(4,128)(2,1)S(1)} reduce(bf16[4,1,79872]{2,0,1:T(4,128)(2,1)S(1)} %maximum_bitcast_fusion, bf16[]{:T(256)} %broadcast.1402), dimensions={1}, to_apply=%copy.185.reduce_sub_computation | reduce | bytes 1277954 | tf_op jit(solution)/shard_map/all_to_all | solution.py:237
  5.5 1.3 reshape.1494
  6.8 4.8 %all-to-all-start = ((bf16[4,2,39936]{2,1,0:T(2,128)(2,1)}), bf16[4,2,39936]{2,1,0:T(2,128)(2,1)S(1)}, u32[]{:S(2)}, u32[]{:S(2)}) async-start(bf16[4,2,39936]{2,1,0:T(2,128)(2,1)} %reshape.1494), calls=%async_computation | async-start | bytes 1277952 | tf_op jit(solution)/shard_map/all_to_all | solution.py:237
  12.7 0.6 fusion.160
  17.3 0.8 convolution_bitcast_fusion.24
  18.1 0.6 slice_bitcast_fusion.9
  18.7 0.5 all-to-all-done
  19.2 0.7 reshape.1495
  19.9 0.5 copy.422
  20.7 0.7 copy.226.refs_1_
  21.5 1.0 fusion.181
  22.6 0.4 cos.128
  23.2 0.7 slice_bitcast_fusion.13
  23.9 0.7 slice_bitcast_fusion.4
  24.6 0.6 slice_bitcast_fusion.25
  25.2 0.6 slice_bitcast_fusion.24
  25.9 0.6 slice_bitcast_fusion.23
  26.5 0.6 copy.421
  27.1 0.8 reshape.1413
  28.0 0.8 fusion.180
  28.8 0.7 multiply_convert_fusion.1
  30.2 0.4 convolution_bitcast_fusion.10
  31.3 0.4 convolution_bitcast_fusion.8
  32.3 0.7 negate_multiply_fusion.2
  33.8 0.4 convolution_bitcast_fusion.6
  34.9 0.4 convolution_bitcast_fusion.4
  35.9 0.7 negate_multiply_fusion.1
  37.4 0.4 convolution_bitcast_fusion.2
  38.5 0.4 convolution_bitcast_fusion
  39.5 0.7 negate_multiply_fusion
  40.5 0.7 fusion.39
  43.7 0.7 fusion.41
  44.7 0.5 convolution_bitcast_fusion.19
  46.9 0.7 fusion.43
  49.8 0.7 fusion.32
  50.8 3.8 %reshape.1408 = f32[16,4,8,8,2,32]{5,4,3,2,0,1:T(2,128)} reshape(f32[16,4,64,64]{3,2,0,1:T(8,128)S(1)} %pad_maximum_fusion) | data formatting | bytes 2097152 | tf_op jit(solution)/shard_map/reshape | solution.py:287
  54.5 6.8 %copy.420 = f32[16,4,8,8,2,32]{5,1,0,2,3,4:T(4,128)} copy(f32[16,4,8,8,2,32]{5,4,3,2,0,1:T(2,128)} %reshape.1408) | data formatting | bytes 2097152 | tf_op jit(solution)/shard_map/reshape | solution.py:287
  61.4 4.5 %reshape.1409.refs_0_ = f32[2,8,8,16,128]{4,3,2,1,0:T(8,128)} reshape(f32[2,8,8,16,4,32]{5,4,3,2,1,0:T(4,128)} %bitcast.534) | data formatting | bytes 2097152 | tf_op jit(solution)/shard_map/reshape | solution.py:289
  65.9 59.6 %shard_map.77 = (f32[64,128]{1,0:T(8,128)}, f32[64,64]{1,0:T(8,128)}) custom-call(f32[2,8,8,16,128]{4,3,2,1,0:T(8,128)} %reshape.1409.refs_0_, f32[64,128]{1,0:T(8,128)} %copy.226.refs_1_), custom_call_target="tpu_custom_call" | custom-call | tf_op jit(solution)/shard_map/pallas_call | solution.py:201
  125.5 6.6 %cholesky.15 = f32[64,64]{1,0:T(8,128)S(1)} custom-call(f32[64,64]{1,0:T(8,128)} %get-tuple-element.4), custom_call_target="Cholesky" | custom-call | tf_op jit(solution)/shard_map/cholesky | solution.py:300
  132.1 0.6 compare_reduce_fusion
  132.8 0.7 fusion.147
  133.4 0.7 copy.227
  134.1 4.9 %custom-call.5 = f32[1,64,64]{1,2,0:T(8,128)S(1)} custom-call(f32[1,64,64]{2,1,0:T(8,128)S(1)} %get-tuple-element.126), custom_call_target="InvertDiagBlocksLowerTriangular" | custom-call | tf_op jit(solution)/shard_map/triangular_solve | solution.py:301
  139.0 1.7 %convolution_bitcast_fusion.28 = f32[64,1,32]{0,2,1:T(8,128)} fusion(f32[1,64,64]{1,2,0:T(8,128)S(1)} %custom-call.5, f32[64,128]{1,0:T(8,128)} %get-tuple-element.5, s32[]{:T(128)S(6)} %select_n.285), kind=kOutput, calls=%fused_computation.32 | convolution fusion | flops 1572864 | bytes 57348 | tf_op jit(solution)/shard_map/triangular_solve | solution.py:301
  (123 shorter events, 16.4 us)
Async XLA Ops:
  0.6 2.4 %copy-start.14 = (f32[1,4096]{1,0:T(1,128)S(1)}, f32[1,4096]{1,0:T(1,128)}, u32[]{:S(2)}) copy-start(f32[1,4096]{1,0:T(1,128)} %param.10) | copy-start | bytes 49156
  5.5 7.2 %copy-start.15 = (f32[8]{0:T(128)S(1)}, f32[8]{0:T(128)}, u32[]{:S(2)}) copy-start(f32[8]{0:T(128)} %param.9) | copy-start | bytes 100
  5.5 10.2 %copy-start.7 = (f32[1,4,2,4096]{3,2,1,0:T(2,128)S(1)}, f32[1,4,2,4096]{3,2,1,0:T(2,128)}, u32[]{:S(2)}) copy-start(f32[1,4,2,4096]{3,2,1,0:T(2,128)} %param.6) | copy-start | bytes 393220
  6.8 12.4 %all-to-all-start = ((bf16[4,2,39936]{2,1,0:T(2,128)(2,1)}), bf16[4,2,39936]{2,1,0:T(2,128)(2,1)S(1)}, u32[]{:S(2)}, u32[]{:S(2)}) async-start(bf16[4,2,39936]{2,1,0:T(2,128)(2,1)} %reshape.1494), calls=%async_computation | async-start | bytes 1277952 | tf_op jit(solution)/shard_map/all_to_all | solution.py:237
  31.3 0.8 copy-start.5
  31.3 0.8 copy-start.6
  34.9 0.8 copy-start.3
  34.9 0.8 copy-start.4
  38.5 0.8 copy-start.1
  38.5 0.8 copy-start.2
  40.4 0.8 copy-start.12
  40.4 0.8 copy-start.13
  41.9 0.8 copy-start
  43.7 0.8 copy-start.10
  43.7 0.8 copy-start.11
  46.9 0.8 copy-start.8
  46.9 0.8 copy-start.9

commit v8 on v7

--- a/solution.py
+++ b/solution.py
@@ -280,7 +280,14 @@
         )
         pieces[plane] = jnp.sum(product_terms, axis=0)
         if plane > 0:
-            turned_back = complex_times(conjugate(plane_screens[:, plane])[:, None], adjoint)
+            screen = plane_screens[:, plane][:, None]
+            turned_back = jnp.stack(
+                [
+                    screen[..., 0, :, :] * adjoint[..., 0, :, :] + screen[..., 1, :, :] * adjoint[..., 1, :, :],
+                    screen[..., 0, :, :] * adjoint[..., 1, :, :] - screen[..., 1, :, :] * adjoint[..., 0, :, :],
+                ],
+                axis=-3,
+            )
             adjoint = propagate(turned_back, spectra_back[:, None], forward, inverse)
     sketch_part = lax.optimization_barrier(jnp.stack(pieces, axis=1))
     rows, planes = sketch_part.shape[0], sketch_part.shape[1]

time: 142 us -> 142 us (level)
  other arithmetic: 29.8 us -> 32 us
    mul x4 -> x1, local copies, waits for them, and re-layouts: 2.49 us -> 0.6 us  [complex_times(): first[..., 0, :, :] * second[..., 0, :, :]]
    unnamed x38 -> x37, local copies, waits for them, and re-layouts: 5.27 us -> 6.31 us
    another operation x19 -> x22, other arithmetic: 3.96 us -> 4.45 us
where the time goes in v8:
time: 142 us; the launch traced here: 141 us
  Pallas kernels  59.3 us (42%)
  other arithmetic  32 us (23%)
  local copies, waits for them, and re-layouts  28.2 us (20%)
  matrix products  12.4 us (9%)
  starting transfers between devices  4.84 us (3%)
  between operations  3.92 us (3%)
    pallas_call x1, Pallas kernels, reduce_all(): pl.pallas_call(lambda *refs: reduce_kernel(stages, depth_size, divisor, r...  59.3 us
    reshape x2, local copies, waits for them, and re-layouts, shards(): by_axes = sketch_part.reshape(rows, planes, CHIPS_Y, CHIPS_Z, CORES, -1)  10.6 us
    another operation x3, other arithmetic, shards(): lower_factor = lax.linalg.cholesky(gram_matrix, symmetrize_input=False)  7.27 us
    unnamed x37, local copies, waits for them, and re-layouts  6.31 us
    dot_general x14, matrix products, transform(): jnp.einsum('nscb,sbtd->ntdc', turned, matrix, preferred_element_type=jnp....  6.19 us
    another operation x1, other arithmetic, shards(): lax.linalg.triangular_solve(lower_factor, flattened, left_side=True, lowe...  4.89 us
    all_to_all x1, starting transfers between devices, shards(): payload = lax.all_to_all(payload, 'depth', 0, 0, tiled=True)  4.84 us
    reshape x1, local copies, waits for them, and re-layouts, shards(): jnp.transpose(by_axes, (4, 3, 2, 0, 1, 5))  4.56 us
  transfers between devices with their start and end apart: 1, of which 1 were waited for; matrix products, arithmetic and copies ran while one was open for 3% of the time, Pallas kernels for 0%

profile of v8, /device:TPU:1, one launch (start us, length us, event | category | flops | bytes accessed | tf_op | source)
XLA Modules:
  0.0 141.1 jit_solution(5861481518426946032)
XLA Ops:
  0.6 1.4 %reshape.1380 = bf16[4,65536]{1,0:T(4,128)(2,1)S(1)} reshape(bf16[64,1,4096]{2,0,1:T(8,128)(2,1)} %param.11) | data formatting | bytes 1048576 | tf_op jit(solution)/shard_map/reshape | solution.py:234
  2.1 0.8 constant_dynamic-slice_fusion
  3.5 0.5 broadcast.1402
  4.0 1.5 %reduce.13 = bf16[4,79872]{1,0:T(4,128)(2,1)S(1)} reduce(bf16[4,1,79872]{2,0,1:T(4,128)(2,1)S(1)} %maximum_bitcast_fusion, bf16[]{:T(256)} %broadcast.1402), dimensions={1}, to_apply=%copy.185.reduce_sub_computation | reduce | bytes 1277954 | tf_op jit(solution)/shard_map/all_to_all | solution.py:237
  5.5 1.2 reshape.1485
  6.8 4.8 %all-to-all-start = ((bf16[4,2,39936]{2,1,0:T(2,128)(2,1)}), bf16[4,2,39936]{2,1,0:T(2,128)(2,1)S(1)}, u32[]{:S(2)}, u32[]{:S(2)}) async-start(bf16[4,2,39936]{2,1,0:T(2,128)(2,1)} %reshape.1485), calls=%async_computation | async-start | bytes 1277952 | tf_op jit(solution)/shard_map/all_to_all | solution.py:237
  12.7 0.6 fusion.161
  17.3 0.8 convolution_bitcast_fusion.24
  18.1 0.6 slice_bitcast_fusion.3
  18.7 0.5 all-to-all-done
  19.1 0.7 reshape.1486
  19.9 0.5 copy.422
  20.4 0.6 slice_convert_fusion.1
  21.0 1.1 fusion.182
  22.2 0.4 sin.149
  22.8 0.6 fusion.90
  23.4 0.7 slice_bitcast_fusion.6
  24.2 0.6 copy.421
  24.8 0.8 reshape.1404
  25.7 0.8 fusion.181
  26.5 0.8 multiply_convert_fusion.1
  28.0 0.4 convolution_bitcast_fusion.10
  29.1 0.4 convolution_bitcast_fusion.8
  30.1 0.7 negate_multiply_fusion.2
  31.6 0.4 convolution_bitcast_fusion.6
  32.7 0.4 convolution_bitcast_fusion.4
  33.7 0.7 negate_multiply_fusion.1
  35.2 0.4 convolution_bitcast_fusion.2
  36.3 0.4 convolution_bitcast_fusion
  37.3 0.7 negate_multiply_fusion
  38.2 0.7 fusion.39
  41.5 0.7 fusion.41
  42.8 0.6 convolution_bitcast_fusion.18
  44.1 0.4 convolution_bitcast_fusion.16
  44.6 1.5 %fusion.43 = f32[16,1,64,64]{3,2,0,1:T(8,128)} fusion(f32[1,16,2,64,64]{4,3,1,2,0:T(8,128)S(1)} %convolution_bitcast_fusion.16, f32[64,64]{1,0:T(8,128)S(1)} %get-tuple-element.99, f32[64,64]{1,0:T(8,128)S(1)} %get-tuple-element.100, f32[]{:T(128)} %fusion.161), kind=kLoop, calls=%fused_computation.144 | loop fusion | flops 262144 | bytes 819204 | tf_op jit(solution)/shard_map/mul | solution.py:278
  46.2 0.6 copy-done.12
  47.0 0.7 copy.226.refs_1_
  50.1 0.8 fusion.32
  51.4 3.8 %reshape.1399 = f32[16,4,8,8,2,32]{5,4,3,2,0,1:T(2,128)} reshape(f32[16,4,64,64]{3,2,0,1:T(8,128)S(1)} %pad_maximum_fusion) | data formatting | bytes 2097152 | tf_op jit(solution)/shard_map/reshape | solution.py:294
  55.2 6.9 %copy.420 = f32[16,4,8,8,2,32]{5,1,0,2,3,4:T(4,128)} copy(f32[16,4,8,8,2,32]{5,4,3,2,0,1:T(2,128)} %reshape.1399) | data formatting | bytes 2097152 | tf_op jit(solution)/shard_map/reshape | solution.py:294
  62.0 4.6 %reshape.1400.refs_0_ = f32[2,8,8,16,128]{4,3,2,1,0:T(8,128)} reshape(f32[2,8,8,16,4,32]{5,4,3,2,1,0:T(4,128)} %bitcast.510) | data formatting | bytes 2097152 | tf_op jit(solution)/shard_map/reshape | solution.py:296
  66.6 59.3 %shard_map.77 = (f32[64,128]{1,0:T(8,128)}, f32[64,64]{1,0:T(8,128)}) custom-call(f32[2,8,8,16,128]{4,3,2,1,0:T(8,128)} %reshape.1400.refs_0_, f32[64,128]{1,0:T(8,128)} %copy.226.refs_1_), custom_call_target="tpu_custom_call" | custom-call | tf_op jit(solution)/shard_map/pallas_call | solution.py:201
  125.9 6.6 %cholesky.15 = f32[64,64]{1,0:T(8,128)S(1)} custom-call(f32[64,64]{1,0:T(8,128)} %get-tuple-element.4), custom_call_target="Cholesky" | custom-call | tf_op jit(solution)/shard_map/cholesky | solution.py:307
  132.6 0.6 compare_reduce_fusion
  133.2 0.7 fusion.148
  133.9 0.7 copy.227
  134.6 4.9 %custom-call.5 = f32[1,64,64]{1,2,0:T(8,128)S(1)} custom-call(f32[1,64,64]{2,1,0:T(8,128)S(1)} %get-tuple-element.110), custom_call_target="InvertDiagBlocksLowerTriangular" | custom-call | tf_op jit(solution)/shard_map/triangular_solve | solution.py:308
  139.5 1.7 %convolution_bitcast_fusion.28 = f32[64,1,32]{0,2,1:T(8,128)} fusion(f32[1,64,64]{1,2,0:T(8,128)S(1)} %custom-call.5, f32[64,128]{1,0:T(8,128)} %get-tuple-element.5, s32[]{:T(128)S(6)} %select_n.285), kind=kOutput, calls=%fused_computation.32 | convolution fusion | flops 1572864 | bytes 57348 | tf_op jit(solution)/shard_map/triangular_solve | solution.py:308
  (113 shorter events, 16.3 us)
Async XLA Ops:
  0.6 2.4 %copy-start.14 = (f32[1,4096]{1,0:T(1,128)S(1)}, f32[1,4096]{1,0:T(1,128)}, u32[]{:S(2)}) copy-start(f32[1,4096]{1,0:T(1,128)} %param.10) | copy-start | bytes 49156
  5.5 7.2 %copy-start.15 = (f32[8]{0:T(128)S(1)}, f32[8]{0:T(128)}, u32[]{:S(2)}) copy-start(f32[8]{0:T(128)} %param.9) | copy-start | bytes 100
  5.5 10.2 %copy-start.13 = (f32[1,4,2,4096]{3,2,1,0:T(2,128)S(1)}, f32[1,4,2,4096]{3,2,1,0:T(2,128)}, u32[]{:S(2)}) copy-start(f32[1,4,2,4096]{3,2,1,0:T(2,128)} %param.6) | copy-start | bytes 393220
  6.8 12.4 %all-to-all-start = ((bf16[4,2,39936]{2,1,0:T(2,128)(2,1)}), bf16[4,2,39936]{2,1,0:T(2,128)(2,1)S(1)}, u32[]{:S(2)}, u32[]{:S(2)}) async-start(bf16[4,2,39936]{2,1,0:T(2,128)(2,1)} %reshape.1485), calls=%async_computation | async-start | bytes 1277952 | tf_op jit(solution)/shard_map/all_to_all | solution.py:237
  26.5 1.3 copy-start.8
  26.5 1.3 copy-start.10
  29.1 0.8 copy-start.2
  29.1 0.8 copy-start.3
  32.7 0.8 copy-start.4
  32.7 0.8 copy-start.5
  36.3 0.8 copy-start.6
  36.3 0.8 copy-start.7
  39.6 0.8 copy-start.1
  46.1 0.8 copy-start.12
  49.3 0.8 copy-start.9
  49.3 0.8 copy-start.11
  50.1 1.0 copy-start
